TPU v7x, 256 devices: a whole 4x4x8 slice. The times are simulated.
256 devices in a mesh: star: 64 (over y, z_lo, x, core), gas: 4 (over z_hi).
Axes of the slice: x: 4, y: 4, z: 8 (z_hi: 4, z_lo: 2; z = z_hi * 2 + z_lo), core: 2. Of those that a mesh axis runs over, the one named last changes fastest.
Arguments:
- star_pos: float32 [3, 131072], P(None, ('star', 'gas')), may hold values from 0 to 32
- star_vel: float32 [3, 131072], P(None, ('star', 'gas')), may hold values from -6 to 6
- star_accel: float32 [6, 131072], P(None, ('star', 'gas')), may hold values from -6 to 6
- star_mass: float32 [131072], P(('star', 'gas')), may hold values from 0.1 to 2
- active: int32 [2048], replicated, may hold values from 0 to 131071, as said below
- density: float32 [256, 32, 64], P('star', 'gas'), may hold values from 0.5 to 4
- flow_in: float32 [3, 256, 32, 64], P(None, 'star', 'gas'), may hold values from -2 to 2
- field_in: float32 [3, 256, 32, 64], P(None, 'star', 'gas'), may hold values from -4 to 4
Outputs:
- star_new: float32 [12, 131072], P(None, ('star', 'gas'))
- flow: float32 [3, 256, 32, 64], P(None, 'star', 'gas')
- field_out: float32 [3, 256, 32, 64], P(None, 'star', 'gas')
Inputs may be any that keep to these rules, and one draw needn't show every extreme that they name: Distinct and increasing; among the 512 consecutive indices of one device at most 24 are active, and in every draw some device holds exactly 24.
All inputs are finite; a program needn't handle non-finite values.
Results may differ from a plain program's by a relative error of at most 0.0001.
Values sent between devices are 32-bit elements; how exact they have to be, the bound alone decides.
A program may use at most 64 MiB of HBM per device.

v0:
```python
import math

import jax
import jax.numpy as jnp
from jax import lax
from jax.sharding import PartitionSpec as P

MOST = 24


gravity = 0.02
soften = 4.0
time_step = 1.5
field_step = 0.1
highest = lax.Precision.HIGHEST


def with_halo(block, sides, width):
    for axis, dim in sides:
        count = lax.axis_size(axis)
        forward = [(i, i + 1) for i in range(count - 1)]
        forward.append((count - 1, 0))
        backward = [(target, source) for source, target in forward]
        low = lax.ppermute(
            lax.slice_in_dim(block, block.shape[dim] - width, None, axis=dim), axis, forward
        )
        high = lax.ppermute(lax.slice_in_dim(block, 0, width, axis=dim), axis, backward)
        block = jnp.concatenate([low, block, high], axis=dim)
    return block


def grad_x(values):
    return 0.5 * (values[2:, 1:-1] - values[:-2, 1:-1])


def grad_y(values):
    return 0.5 * (values[1:-1, 2:] - values[1:-1, :-2])


def grad_z(values):
    return 0.5 * (jnp.roll(values, -1, 2) - jnp.roll(values, 1, 2))[1:-1, 1:-1]


def trim_rim(values):
    return values[1:-1, 1:-1]


def curl_of(comp_a, comp_b, comp_c):
    return (
        grad_y(comp_c) - grad_z(comp_b),
        grad_z(comp_a) - grad_x(comp_c),
        grad_x(comp_b) - grad_y(comp_a),
    )


def cross_of(lhs_vec, rhs_vec):
    return (
        lhs_vec[1] * rhs_vec[2] - lhs_vec[2] * rhs_vec[1],
        lhs_vec[2] * rhs_vec[0] - lhs_vec[0] * rhs_vec[2],
        lhs_vec[0] * rhs_vec[1] - lhs_vec[1] * rhs_vec[0],
    )


def field_rate(padded_field, padded_flow, padded_density):
    current = curl_of(padded_field[0], padded_field[1], padded_field[2])
    inner_field = (trim_rim(padded_field[0]), trim_rim(padded_field[1]), trim_rim(padded_field[2]))
    inner_flow = (trim_rim(padded_flow[0]), trim_rim(padded_flow[1]), trim_rim(padded_flow[2]))
    resist = trim_rim(padded_density) ** (-1.5)
    lorentz = cross_of(current, inner_field)
    drift = cross_of(lorentz, inner_field)
    motion = cross_of(inner_flow, inner_field)
    emf_a = motion[0] + resist * drift[0]
    emf_b = motion[1] + resist * drift[1]
    emf_c = motion[2] + resist * drift[2]
    return jnp.stack(curl_of(emf_a, emf_b, emf_c))


def pair_terms(target, resident, cell_place, cell_mass):
    star_gap = resident[0:3, None, :] - target[0:3, :, None]
    rel_vel = resident[3:6, None, :] - target[3:6, :, None]
    inv_r = lax.rsqrt(jnp.sum(star_gap * star_gap, 0) + soften)
    weight = gravity * resident[6][None, :] * inv_r * inv_r * inv_r
    star_acc = jnp.sum(weight[None] * star_gap, 2)
    approach = jnp.sum(star_gap * rel_vel, 0)
    star_jerk = jnp.sum(
        weight[None] * (rel_vel - 3.0 * (approach * inv_r * inv_r)[None] * star_gap), 2
    )
    cell_gap = cell_place[:, None, :] - target[0:3, :, None]
    inv_g = lax.rsqrt(jnp.sum(cell_gap * cell_gap, 0) + soften)
    inv_cube = gravity * inv_g * inv_g * inv_g
    gas_acc = jnp.sum((inv_cube * cell_mass[None, :])[None] * cell_gap, 2)
    cell_kick = -jnp.sum((inv_cube * target[6][:, None])[None] * cell_gap, 1)
    return (jnp.concatenate([star_acc + gas_acc, star_jerk], 0), cell_kick)


def all_terms(targets, resident, cell_place, cell_mass):
    target_total = targets.shape[1]
    block_width = math.gcd(target_total, 64)
    blocks = targets.reshape(7, target_total // block_width, block_width).transpose(1, 0, 2)

    def one_block(running, target_block):
        terms_here, cell_kick = pair_terms(target_block, resident, cell_place, cell_mass)
        return (running + cell_kick, terms_here)

    kick_sum, block_terms = lax.scan(one_block, jnp.zeros(cell_place.shape, jnp.float32), blocks)
    return (block_terms.transpose(1, 0, 2).reshape(6, target_total), kick_sum)


def body(star_pos, star_vel, star_accel, star_mass, active, density, flow_in, field_in):
    resident_total = star_pos.shape[1]
    old_acc = star_accel[0:3]
    old_jerk = star_accel[3:6]
    pred_pos = (
        star_pos
        + time_step * star_vel
        + time_step**2 / 2.0 * old_acc
        + time_step**3 / 6.0 * old_jerk
    )
    pred_vel = star_vel + time_step * old_acc + time_step**2 / 2.0 * old_jerk
    resident = jnp.concatenate([pred_pos, pred_vel, star_mass[None]], 0)
    my_rank = lax.axis_index("star") * lax.axis_size("gas") + lax.axis_index("gas")
    owner_of = active // resident_total
    local_slot = active % resident_total
    is_mine = owner_of == my_rank
    rows_iota = jnp.arange(resident_total, dtype=jnp.int32)
    owned = (is_mine[None, :] & (local_slot[None, :] == rows_iota[:, None])).astype(jnp.float32)
    active_mask = jnp.sum(owned, 1) > 0.5
    ext_x, ext_y, ext_z = density.shape
    grid_shape = (ext_x, ext_y, ext_z)
    coord_x = (lax.axis_index("star") * ext_x + jnp.arange(ext_x)).astype(jnp.float32) + 0.5
    coord_y = (lax.axis_index("gas") * ext_y + jnp.arange(ext_y)).astype(jnp.float32) + 0.5
    coord_z = jnp.arange(ext_z).astype(jnp.float32) + 0.5
    cell_place = jnp.stack(
        [
            jnp.broadcast_to(coord_x[:, None, None], grid_shape),
            jnp.broadcast_to(coord_y[None, :, None], grid_shape),
            jnp.broadcast_to(coord_z[None, None, :], grid_shape),
        ]
    ).reshape(3, -1)
    cell_mass = density.reshape(-1)
    order_rank = jnp.cumsum(is_mine.astype(jnp.int32)) - 1
    slot_iota = jnp.arange(MOST, dtype=jnp.int32)
    slot_pick = (is_mine[:, None] & (order_rank[:, None] == slot_iota[None, :])).astype(jnp.float32)
    selector = jnp.dot(owned, slot_pick, precision=highest)
    packed = jnp.dot(resident, selector, precision=highest)
    targets = lax.all_gather(packed, ("star", "gas"), axis=1, tiled=True)
    partial_terms, kick_sum = all_terms(targets, resident, cell_place, cell_mass)
    summed = lax.psum(partial_terms, ("star", "gas"))
    mine_terms = lax.dynamic_slice_in_dim(summed, my_rank * MOST, MOST, 1)
    own_terms = jnp.dot(mine_terms, selector.T, precision=highest)
    new_acc = own_terms[0:3]
    new_jerk = own_terms[3:6]
    vel_one = (
        star_vel
        + time_step * (old_acc + new_acc) / 2.0
        + time_step**2 * (old_jerk - new_jerk) / 12.0
    )
    pos_one = (
        star_pos
        + time_step * (star_vel + vel_one) / 2.0
        + time_step**2 * (old_acc - new_acc) / 12.0
    )
    updated = jnp.concatenate([pos_one, vel_one, new_acc, new_jerk], 0)
    base = jnp.concatenate([star_pos, star_vel, star_accel], 0)
    star_new = jnp.where(active_mask[None, :], updated, base)
    flow = flow_in + time_step * kick_sum.reshape(3, ext_x, ext_y, ext_z)

    def rate_of(values):
        padded = with_halo(
            jnp.concatenate([values, flow, density[None]], 0), (("star", 1), ("gas", 2)), 2
        )
        return field_rate(padded[0:3], padded[3:6], padded[6])

    first_section = field_in + field_step * rate_of(field_in)
    field_out = 0.5 * (field_in + first_section + field_step * rate_of(first_section))
    return (star_new, flow, field_out)


def solution(mesh):
    placed = (
        P(None, ("star", "gas")),
        P(None, ("star", "gas")),
        P(None, ("star", "gas")),
        P(("star", "gas")),
        P(),
        P("star", "gas", None),
        P(None, "star", "gas", None),
        P(None, "star", "gas", None),
    )
    return jax.shard_map(
        body,
        mesh=mesh,
        in_specs=placed,
        out_specs=(
            P(None, ("star", "gas")),
            P(None, "star", "gas", None),
            P(None, "star", "gas", None),
        ),
        check_vma=False,
    )
```

profile of v0, /device:TPU:32, one launch (start us, length us, event | category | flops | bytes accessed | tf_op | source)
XLA Modules:
  0.0 1056.4 jit_solution(8387592304197424626)
XLA Ops:
  7.3 0.7 add_select_fusion
  8.0 0.7 convert_bitcast_fusion
  9.3 1.4 fusion.14
  10.9 612.3 %all-gather = f32[256,24,7]{1,2,0:T(8,128)S(1)} all-gather(f32[1,24,7]{1,2,0:T(8,128)S(1)} %convolution_bitcast_fusion), channel_id=1, replica_groups=mesh['star'=64,'gas'=4] {'star','gas'}, dimensions={0}, use_global_device_ids=true | all-gather | bytes 172704 | tf_op jit(solution)/shard_map/all_gather | solution.py:146
  623.4 0.5 reshape.159
  624.8 144.5 %while.14 = (s32[]{:T(128)}, f32[3,2048]{1,0:T(4,128)S(1)}, f32[96,6,64]{2,1,0:T(8,128)S(1)}, f32[3,4,8,64]{3,2,1,0:T(8,128)}, f32[96,7,64]{2,0,1:T(8,128)S(1)},...) while((s32[]{:T(128)}, f32[3,2048]{1,0:T(4,128)S(1)}, ...), condition=%wide.wide.region_11.12_spmd.clone, body=%wide.wide.region_3.11_spmd.clone.sunk | while | flops 5353989 | bytes 4405187 | solution.py:105
  625.7 0.5 fusion.148
  627.3 0.5 fusion.148
  628.8 0.5 fusion.148
  769.5 0.7 pad_maximum_fusion.9
  770.4 3.8 collective-permute-start.1
  774.3 0.8 reshape.156
  775.1 0.8 convert_reduce_fusion
  776.2 4.1 collective-permute-start.3
  780.4 2.1 collective-permute-done.2
  783.8 3.8 collective-permute-start.5
  787.6 251.2 %all-reduce.2.cloned.1.call-done = f32[6,6144]{1,0:T(8,128)} async-done(((f32[6,6144]{1,0:T(8,128)}), f32[6,6144]{1,0:T(8,128)}) %all-reduce.2.cloned.1.call-update) | async-done | bytes 147472 | tf_op jit(solution)/shard_map/psum | solution.py:148
  1038.8 0.9 fusion.97
  1039.8 1.7 collective-permute-start.6
  1041.5 2.5 collective-permute-start.7
  1044.0 0.6 maximum_select_fusion
  1044.7 1.9 collective-permute-done.6
  1046.5 1.2 collective-permute-done.7
  1049.0 0.6 fusion.58
  (1337 shorter events, 139.8 us)
Async XLA Ops:
  7.2 1031.6 %all-reduce.2.cloned.1.call-start = ((), (), s32[]{:S(2)}) async-start(), calls=%async_computation | async-start | bytes 393216 | tf_op jit(solution)/shard_map/psum | solution.py:148
  9.3 1.4 copy-start.5
  9.3 1.4 copy-start.7
  9.3 1.4 copy-start.8
  9.3 1.5 copy-start.6
  623.3 1.0 copy-start.2
  624.2 0.6 copy-start.4
  624.8 144.7 %copy-start.9 = (f32[3,4,8,64]{3,2,1,0:T(8,128)S(1)}, f32[3,4,8,64]{3,2,1,0:T(8,128)}, u32[]{:S(2)}) copy-start(f32[3,4,8,64]{3,2,1,0:T(8,128)} %param.16) | copy-start | bytes 73732
  624.8 144.7 %copy-start.1 = (f32[3,4,8,64]{3,2,1,0:T(8,128)S(1)}, f32[3,4,8,64]{3,2,1,0:T(8,128)}, u32[]{:S(2)}) copy-start(f32[3,4,8,64]{3,2,1,0:T(8,128)} %param.17) | copy-start | bytes 73732
  769.4 6.7 copy-start.3
  769.5 278.2 %copy-start = (f32[3,4,8,64]{3,2,1,0:T(8,128)}, f32[3,4,8,64]{3,2,1,0:T(8,128)S(1)}, u32[]{:S(2)}) copy-start(f32[3,4,8,64]{3,2,1,0:T(8,128)S(1)} %add.174) | copy-start | bytes 73732
  770.3 5.8 collective-permute-start
  770.4 5.7 collective-permute-start.1
  776.1 6.4 collective-permute-start.2
  776.2 6.3 collective-permute-start.3
  783.7 256.0 %collective-permute-start.4 = (f32[7,2,8,64]{3,2,1,0:T(8,128)S(1)}, f32[7,2,8,64]{3,2,1,0:T(8,128)S(1)}, u32[]{:S(2)}, u32[]{:S(2)}) collective-permute-start(f32[7,2,8,64]{3,2,1,0:T(8,128)S(1)} %get-tuple-element.178), channel_id=1, source_target_pairs={{0,4},{4,8},{8,12},{12,16},{16,20},{20,24},{24,28},{28,32},{32,36}... | collective-permute-start | bytes 86024 | tf_op jit(solution)/shard_map/ppermute | solution.py:24
  783.8 256.0 %collective-permute-start.5 = (f32[7,2,8,64]{3,2,1,0:T(8,128)S(1)}, f32[7,2,8,64]{3,2,1,0:T(8,128)S(1)}, u32[]{:S(2)}, u32[]{:S(2)}) collective-permute-start(f32[7,2,8,64]{3,2,1,0:T(8,128)S(1)} %get-tuple-element.179), channel_id=1, source_target_pairs={{4,0},{8,4},{12,8},{16,12},{20,16},{24,20},{28,24},{32,28},{36,32}... | collective-permute-start | bytes 86024 | tf_op jit(solution)/shard_map/ppermute | solution.py:27
  1039.8 6.7 collective-permute-start.6
  1041.5 6.2 collective-permute-start.7
Sparse Core Ops, SparseCore 0:
  775.2 263.5 all-reduce.1
where the time goes:
time: 1060 us
  blocking collectives  612 us (58%)
  waiting for transfers between devices  257 us (24%)
  other arithmetic  139 us (13%)
  starting transfers between devices  16.3 us (2%)
  between operations  14.4 us (1%)
    all_gather x1, blocking collectives, body(): targets = lax.all_gather(packed, ('star', 'gas'), axis=1, tiled=True)  612 us
    psum x1, waiting for transfers between devices, body(): summed = lax.psum(partial_terms, ('star', 'gas'))  251 us
    reduce_sum x96, other arithmetic, pair_terms(): gas_acc = jnp.sum((inv_cube * cell_mass[None, :])[None] * cell_gap, 2)  48.2 us
    reduce_sum x96, other arithmetic, pair_terms(): star_acc = jnp.sum(weight[None] * star_gap, 2)  27.3 us
  transfers between devices with their start and end apart: 9, of which 5 were waited for; matrix products, arithmetic and copies ran while one was open for 0% of the time, Pallas kernels for 0%

commit v1 on v0

v1 whole, which is shorter than its diff:
```python
import functools

import jax
import jax.numpy as jnp
from jax import lax
from jax.experimental import pallas as pl
from jax.experimental.pallas import tpu as pltpu
from jax.sharding import PartitionSpec as P

MESH = pl.DeviceIdType.MESH
gravity = 0.02
soften = 4.0
time_step = 1.5
field_step = 0.1

STARS = 512
ACTIVE = 2048
BLOCKS = ACTIVE // 128
XC, ZL, YN, GAS = 8, 2, 4, 4
TILES = YN * ZL * XC
SLOTS = 32
MOST = 24
NXL, NYL, NZ = 4, 8, 64
COLS = NXL * NYL
f32 = jnp.float32
i32 = jnp.int32


def lanes(shape=(8, 128)):
    return lax.broadcasted_iota(i32, shape, len(shape) - 1)


def take_lanes(values, index):
    return jnp.take_along_axis(values, index, axis=1, mode="promise_in_bounds")


def place():
    star = lax.axis_index("star")
    gas = lax.axis_index("gas")
    xc = lax.rem(star, XC)
    zl = lax.rem(lax.div(star, XC), ZL)
    y = lax.div(star, XC * ZL)
    return star, gas, y, zl, xc


def star_of(y, zl, xc):
    return (y * ZL + zl) * XC + xc


def z_peers(y, zl, xc, gas):
    zi = zl * GAS + gas
    peers = []
    for d in range(1, ZL * GAS):
        other = lax.rem(zi + d, ZL * GAS)
        ozl, ogas = lax.div(other, GAS), lax.rem(other, GAS)
        peers.append((other, ozl, (star_of(y, ozl, xc), ogas)))
    return zi, peers


def y_peers(y, zl, xc, gas):
    peers = []
    for d in range(1, YN):
        other = lax.rem(y + d, YN)
        peers.append((other, (star_of(other, zl, xc), gas)))
    return peers


def xc_peers(y, zl, xc, gas):
    peers = []
    for d in range(1, XC):
        other = lax.rem(xc + d, XC)
        peers.append((other, (star_of(y, zl, other), gas)))
    return peers


def meet(devices):
    barrier = pltpu.get_barrier_semaphore()
    for device in devices:
        pl.semaphore_signal(barrier, inc=1, device_id=device, device_id_type=MESH)
    return lambda: pl.semaphore_wait(barrier, len(devices))


def send(src, dst, send_sem, recv_sem, device):
    copy = pltpu.make_async_remote_copy(
        src_ref=src, dst_ref=dst, send_sem=send_sem, recv_sem=recv_sem,
        device_id=device, device_id_type=MESH,
    )
    copy.start()
    return copy


def own_indices(active_ref, rank, lane0):
    act = active_ref[...]
    base = rank * STARS
    begin = jnp.sum((act < base).astype(f32)).astype(i32)
    slot = lanes() - lane0
    t = begin + slot
    inside = (slot >= 0) & (slot < SLOTS) & (t < ACTIVE)
    t = jnp.where(inside, t, 0)
    block, lane = t >> 7, t & 127
    found = jnp.full((8, 128), -1, i32)
    for b in range(BLOCKS):
        row = jnp.broadcast_to(active_ref[b : b + 1, :], (8, 128))
        found = jnp.where(block == b, take_lanes(row, lane), found)
    local = found - base
    used = inside & (local >= 0) & (local < STARS)
    return jnp.where(used, local, -1), used


def gather_kernel(
    pos, vel, accel, mass, active, tiles, res, begins, zbuf, own, zs, zr, ys, yr, xs, xr
):
    star, gas, y, zl, xc = place()
    zi, zp = z_peers(y, zl, xc, gas)
    yp = y_peers(y, zl, xc, gas)
    xp = xc_peers(y, zl, xc, gas)
    arrived = meet([p[-1] for p in zp] + [p[-1] for p in yp] + [p[-1] for p in xp])
    old_acc, old_jerk = accel[0:3, :], accel[3:6, :]
    v = vel[...]
    res[0:3, :] = (
        pos[...] + time_step * v + time_step**2 / 2.0 * old_acc + time_step**3 / 6.0 * old_jerk
    )
    res[3:6, :] = v + time_step * old_acc + time_step**2 / 2.0 * old_jerk
    res[6:7, :] = mass[...]
    res[7:8, :] = jnp.zeros((1, STARS), f32)
    local, used = own_indices(active, star * GAS + gas, gas * SLOTS)
    block, lane = local >> 7, local & 127
    packed = jnp.zeros((8, 128), f32)
    for b in range(STARS // 128):
        packed = jnp.where(
            used & (block == b), take_lanes(res[:, b * 128 : (b + 1) * 128], lane), packed
        )
    own[...] = packed
    zbuf[zi] = packed
    arrived()
    zc = [
        send(own, zbuf.at[zi], zs.at[d], zr.at[d], device)
        for d, (other, ozl, device) in enumerate(zp)
    ]
    edge0 = (lanes((128, 128)) * STARS).astype(f32)
    edge1 = edge0 + 128.0 * STARS
    count0 = jnp.zeros((8, 128), f32)
    count1 = jnp.zeros((8, 128), f32)
    for b in range(BLOCKS):
        row = jnp.broadcast_to(active[b : b + 1, :].astype(f32), (128, 128))
        col = jnp.transpose(row)
        less0 = jnp.where(col < edge0, 1.0, 0.0).reshape(16, 8, 128)
        less1 = jnp.where(col < edge1, 1.0, 0.0).reshape(16, 8, 128)
        count0 = count0 + jnp.sum(less0, 0)
        count1 = count1 + jnp.sum(less1, 0)
    begins[0:1, :] = jnp.sum(count0, 0, keepdims=True).astype(i32)
    begins[1:2, :] = jnp.sum(count1, 0, keepdims=True).astype(i32)
    for copy in zc:
        copy.wait()
    for z in range(ZL):
        merged = zbuf[z * GAS]
        for g in range(1, GAS):
            merged = merged + zbuf[z * GAS + g]
        tiles[y, z, xc] = merged
    yc = [
        send(tiles.at[y, :, xc], tiles.at[y, :, xc], ys.at[d], yr.at[d], device)
        for d, (other, device) in enumerate(yp)
    ]
    for copy in yc:
        copy.wait()
    xcs = [
        send(tiles.at[:, :, xc], tiles.at[:, :, xc], xs.at[d], xr.at[d], device)
        for d, (other, device) in enumerate(xp)
    ]
    for copy in xcs:
        copy.wait()


def compute_kernel(
    tiles, res, begins, active, density, flow_in, part, flow,
    targ, rb, mb, dz, dz2, mdz, gacc, pt, ks, square
):
    star, gas, y, zl, xc = place()
    lane8 = lanes()
    begin0 = jnp.broadcast_to(begins[0:1, :], (8, 128))
    begin1 = jnp.broadcast_to(begins[1:2, :], (8, 128))

    def compact(b, _):
        act = jnp.broadcast_to(active[pl.ds(b, 1), :], (8, 128))
        owner = act >> 9
        begin = jnp.where(
            owner < 128, take_lanes(begin0, owner & 127), take_lanes(begin1, owner & 127)
        )
        slot = b * 128 + lane8 - begin
        lane = (owner & (GAS - 1)) * SLOTS + slot
        tile = owner >> 2

        def pick(q, found):
            for r in range(8):
                found = jnp.where(tile == q * 8 + r, take_lanes(tiles[q * 8 + r], lane), found)
            return found

        targ[b] = lax.fori_loop(0, TILES // 8, pick, jnp.zeros((8, 128), f32))
        return 0

    lax.fori_loop(0, BLOCKS, compact, 0)

    square[...] = jnp.zeros((128, 128), f32)
    for q in range(STARS // 128):
        square[0:8, :] = res[:, q * 128 : (q + 1) * 128]
        turned = jnp.transpose(square[...])
        for f in range(7):
            column = turned[:, f : f + 1]
            if f == 6:
                column = column * gravity
            rb[f, q * 128 : (q + 1) * 128, :] = jnp.broadcast_to(column, (128, 128))
    for i in range(NXL):
        square[i * NYL : (i + 1) * NYL, 0:NZ] = density[i]
    turned = jnp.transpose(square[...])
    for c in range(COLS):
        mb[c] = jnp.broadcast_to(turned[0:NZ, c : c + 1] * gravity, (NZ, 128)).reshape(8, 8, 128)

    def row(b, f):
        return jnp.broadcast_to(targ[b, f : f + 1, :], (8, 128))

    height = (
        lax.broadcasted_iota(i32, (8, 8, 128), 0) * 8 + lax.broadcasted_iota(i32, (8, 8, 128), 1)
    ).astype(f32) + 0.5

    def stars_on(b, _):
        tx, ty, tz, tu, tv, tw = (row(b, f) for f in range(6))

        def group(g, sums):
            ax, ay, az, jx, jy, jz = sums
            for r in range(4):
                at = pl.ds(pl.multiple_of(g * 32 + r * 8, 8), 8)
                dx, dy, dzz = rb[0, at, :] - tx, rb[1, at, :] - ty, rb[2, at, :] - tz
                ux, uy, uz = rb[3, at, :] - tu, rb[4, at, :] - tv, rb[5, at, :] - tw
                inv = lax.rsqrt(dx * dx + dy * dy + dzz * dzz + soften)
                inv2 = inv * inv
                w = rb[6, at, :] * (inv2 * inv)
                q = 3.0 * (dx * ux + dy * uy + dzz * uz) * inv2
                ax, ay, az = ax + w * dx, ay + w * dy, az + w * dzz
                jx = jx + w * (ux - q * dx)
                jy = jy + w * (uy - q * dy)
                jz = jz + w * (uz - q * dzz)
            return ax, ay, az, jx, jy, jz

        zero = jnp.zeros((8, 128), f32)
        sums = lax.fori_loop(0, STARS // 32, group, (zero,) * 6)
        for f in range(6):
            pt[b, f : f + 1, :] = jnp.sum(sums[f], 0, keepdims=True)
        depth = height - row(b, 2)[None]
        dz[b] = depth
        dz2[b] = depth * depth
        mdz[b] = depth * (row(b, 6) * gravity)[None]
        for f in range(3):
            gacc[f, b] = zero
        return 0

    lax.fori_loop(0, BLOCKS, stars_on, 0)

    for f in range(3):
        ks[f] = jnp.zeros((128, 128), f32)
    x_first = (star * NXL).astype(f32) + 0.5
    y_first = (gas * NYL).astype(f32) + 0.5

    def column(c, _):
        x_here = x_first + lax.div(c, NYL).astype(f32)
        y_here = y_first + lax.rem(c, NYL).astype(f32)
        cell = mb[c]

        def targets_at(b, sums):
            kx, ky, kz = sums
            dx = x_here - row(b, 0)
            dy = y_here - row(b, 1)
            tm = row(b, 6) * gravity
            depth = dz[b]
            inv = lax.rsqrt((dx * dx + dy * dy + soften)[None] + dz2[b])
            w = inv * inv * inv
            u = cell * w
            total = jnp.sum(u, 0)
            gacc[0, b] += total * dx
            gacc[1, b] += total * dy
            gacc[2, b] += jnp.sum(u * depth, 0)
            kx = kx + w * (tm * dx)[None]
            ky = ky + w * (tm * dy)[None]
            kz = kz + w * mdz[b]
            return kx, ky, kz

        zero = jnp.zeros((8, 8, 128), f32)
        sums = lax.fori_loop(0, BLOCKS, targets_at, (zero,) * 3, unroll=2)
        mark = lanes((NZ, 128)) == c
        for f in range(3):
            column_sum = jnp.sum(sums[f].reshape(NZ, 128), 1, keepdims=True)
            ks[f, 0:NZ, :] = jnp.where(mark, column_sum, ks[f, 0:NZ, :])
        return 0

    lax.fori_loop(0, COLS, column, 0)
    for f in range(3):
        turned = jnp.transpose(ks[f])
        for i in range(NXL):
            flow[f, i] = flow_in[f, i] - time_step * turned[i * NYL : (i + 1) * NYL, 0:NZ]

    def close(b, _):
        for f in range(3):
            pt[b, f : f + 1, :] += jnp.sum(gacc[f, b], 0, keepdims=True)
        pt[b, 6:8, :] = jnp.zeros((2, 128), f32)
        return 0

    lax.fori_loop(0, BLOCKS, close, 0)

    def expand(s, _):
        owner = s * GAS + (lane8 >> 5)
        begin = jnp.where(
            owner < 128, take_lanes(begin0, owner & 127), take_lanes(begin1, owner & 127)
        )
        t = jnp.minimum(begin + (lane8 & (SLOTS - 1)), ACTIVE - 1)
        block, lane = t >> 7, t & 127
        found = jnp.zeros((8, 128), f32)
        for b in range(BLOCKS):
            found = jnp.where(block == b, take_lanes(pt[b], lane), found)
        part[s] = found
        return 0

    lax.fori_loop(0, TILES, expand, 0)


def cross_of(lhs, rhs):
    return (
        lhs[1] * rhs[2] - lhs[2] * rhs[1],
        lhs[2] * rhs[0] - lhs[0] * rhs[2],
        lhs[0] * rhs[1] - lhs[1] * rhs[0],
    )


def diff_x(v):
    return 0.5 * (v[2:] - v[:-2])


def diff_y(v):
    n = v.shape[1]
    return (0.5 * (pltpu.roll(v, n - 1, 1) - pltpu.roll(v, 1, 1)))[1:-1]


def diff_z(v):
    n = v.shape[2]
    return (0.5 * (pltpu.roll(v, n - 1, 2) - pltpu.roll(v, 1, 2)))[1:-1]


def curl_of(a, b, c):
    return (diff_y(c) - diff_z(b), diff_z(a) - diff_x(c), diff_x(b) - diff_y(a))


def rate_of(field, flow, resist):
    current = curl_of(*field)
    inner = tuple(v[1:-1] for v in field)
    drift = cross_of(cross_of(current, inner), inner)
    motion = cross_of(flow, inner)
    emf = tuple(m + resist * d for m, d in zip(motion, drift))
    return curl_of(*emf)


def finish_kernel(
    part, field, flow, density, pos, vel, accel, active, star_new, field_out,
    brick, near, r1, q1, r2, t2, r3, big, hs, hr, zs, zr, ys, yr, xs, xr
):
    star, gas, y, zl, xc = place()
    zi, zp = z_peers(y, zl, xc, gas)
    yp = y_peers(y, zl, xc, gas)
    xp = xc_peers(y, zl, xc, gas)
    stars_all = TILES
    sides = []
    for dx in (-1, 0, 1):
        for dy in (-1, 0, 1):
            if dx or dy:
                device = (
                    lax.rem(star + dx + stars_all, stars_all),
                    lax.rem(gas + dy + GAS, GAS),
                )
                sides.append((dx, dy, device))
    arrived = meet(
        [p[-1] for p in zp] + [p[-1] for p in yp] + [p[-1] for p in xp] + [p[-1] for p in sides]
    )
    for f in range(3):
        brick[f] = field[f]
        brick[3 + f] = flow[f]
    brick[6] = density[...]
    arrived()
    xcs = [
        send(part.at[:, :, other], r1.at[xc], xs.at[d], xr.at[d], device)
        for d, (other, device) in enumerate(xp)
    ]
    hcs = [
        send(brick, near.at[1 - dx, 1 - dy], hs.at[d], hr.at[d], device)
        for d, (dx, dy, device) in enumerate(sides)
    ]
    r1[xc] = part[:, :, xc]
    near[1, 1] = brick[...]
    for copy in xcs:
        copy.wait()
    total = r1[0]
    for n in range(1, XC):
        total = total + r1[n]
    q1[...] = total
    ycs = [
        send(q1.at[other], r2.at[y], ys.at[d], yr.at[d], device)
        for d, (other, device) in enumerate(yp)
    ]
    r2[y] = q1[y]
    for copy in ycs:
        copy.wait()
    total = r2[0]
    for n in range(1, YN):
        total = total + r2[n]
    t2[...] = total
    zcs = [
        send(t2.at[ozl], r3.at[zi], zs.at[d], zr.at[d], device)
        for d, (other, ozl, device) in enumerate(zp)
    ]
    r3[zi] = t2[zl]

    for copy in hcs:
        copy.wait()
    for c in range(7):
        for dx in range(3):
            for dy in range(3):
                for i in range(NXL):
                    v = near[dx, dy, c, i]
                    big[c, dx * NXL + i, dy * NYL : (dy + 1) * NYL, :] = jnp.concatenate(
                        [v, v], axis=1
                    )
    mag = tuple(big[c] for c in range(3))
    wind = tuple(big[3 + c] for c in range(3))
    inv = lax.rsqrt(big[6])
    resist = inv * inv * inv
    first = rate_of(mag, tuple(v[1:-1] for v in wind), resist[1:-1])
    one = tuple(m[2:-2] + field_step * r for m, r in zip(mag, first))
    second = rate_of(one, tuple(v[3:-3] for v in wind), resist[3:-3])
    for c in range(3):
        out = 0.5 * (mag[c][4:-4] + one[c][2:-2] + field_step * second[c])
        field_out[c] = out[:, NYL : 2 * NYL, 0:NZ]

    local, used = own_indices(active, star * GAS + gas, 0)
    for copy in zcs:
        copy.wait()
    total = r3[0]
    for n in range(1, ZL * GAS):
        total = total + r3[n]
    mine = pltpu.roll(total, lax.rem(128 - gas * SLOTS, 128), 1)
    index = lanes((8, STARS))
    sums = jnp.zeros((8, STARS), f32)
    hit = jnp.zeros((8, STARS), f32)
    for s in range(MOST):
        here = index == local[:, s : s + 1]
        sums = jnp.where(here, mine[:, s : s + 1], sums)
        hit = jnp.where(here, 1.0, hit)
    is_active = hit[0:3] > 0.5
    new_acc, new_jerk = sums[0:3], sums[3:6]
    p, v = pos[...], vel[...]
    old_acc, old_jerk = accel[0:3, :], accel[3:6, :]
    vel_one = v + time_step * (old_acc + new_acc) / 2.0 + time_step**2 * (old_jerk - new_jerk) / 12.0
    pos_one = p + time_step * (v + vel_one) / 2.0 + time_step**2 * (old_acc - new_acc) / 12.0
    star_new[0:3, :] = jnp.where(is_active, pos_one, p)
    star_new[3:6, :] = jnp.where(is_active, vel_one, v)
    star_new[6:9, :] = jnp.where(is_active, new_acc, old_acc)
    star_new[9:12, :] = jnp.where(is_active, new_jerk, old_jerk)


VM = pl.BlockSpec(memory_space=pltpu.VMEM)
DMA = pltpu.SemaphoreType.DMA


def body(star_pos, star_vel, star_accel, star_mass, active, density, flow_in, field_in):
    act = active.reshape(BLOCKS, 128)
    tiles, res, begins = pl.pallas_call(
        gather_kernel,
        out_shape=(
            jax.ShapeDtypeStruct((YN, ZL, XC, 8, 128), f32),
            jax.ShapeDtypeStruct((8, STARS), f32),
            jax.ShapeDtypeStruct((2, 128), i32),
        ),
        in_specs=[VM] * 5,
        out_specs=(VM,) * 3,
        scratch_shapes=[
            pltpu.VMEM((ZL * GAS, 8, 128), f32),
            pltpu.VMEM((8, 128), f32),
            DMA((ZL * GAS - 1,)), DMA((ZL * GAS - 1,)),
            DMA((YN - 1,)), DMA((YN - 1,)),
            DMA((XC - 1,)), DMA((XC - 1,)),
        ],
        compiler_params=pltpu.CompilerParams(collective_id=0, has_side_effects=True),
        name="gather_targets",
    )(star_pos, star_vel, star_accel, star_mass.reshape(1, STARS), act)
    part, flow = pl.pallas_call(
        compute_kernel,
        out_shape=(
            jax.ShapeDtypeStruct((TILES, 8, 128), f32),
            jax.ShapeDtypeStruct((3, NXL, NYL, NZ), f32),
        ),
        in_specs=[VM] * 6,
        out_specs=(VM,) * 2,
        scratch_shapes=[
            pltpu.VMEM((BLOCKS, 8, 128), f32),
            pltpu.VMEM((7, STARS, 128), f32),
            pltpu.VMEM((COLS, 8, 8, 128), f32),
            pltpu.VMEM((BLOCKS, 8, 8, 128), f32),
            pltpu.VMEM((BLOCKS, 8, 8, 128), f32),
            pltpu.VMEM((BLOCKS, 8, 8, 128), f32),
            pltpu.VMEM((3, BLOCKS, 8, 128), f32),
            pltpu.VMEM((BLOCKS, 8, 128), f32),
            pltpu.VMEM((3, 128, 128), f32),
            pltpu.VMEM((128, 128), f32),
        ],
        compiler_params=pltpu.CompilerParams(vmem_limit_bytes=48 << 20),
        name="pair_sums",
    )(tiles.reshape(TILES, 8, 128), res, begins, act, density, flow_in)
    star_new, field_out = pl.pallas_call(
        finish_kernel,
        out_shape=(
            jax.ShapeDtypeStruct((12, STARS), f32),
            jax.ShapeDtypeStruct((3, NXL, NYL, NZ), f32),
        ),
        in_specs=[VM] * 8,
        out_specs=(VM,) * 2,
        scratch_shapes=[
            pltpu.VMEM((7, NXL, NYL, NZ), f32),
            pltpu.VMEM((3, 3, 7, NXL, NYL, NZ), f32),
            pltpu.VMEM((XC, YN, ZL, 8, 128), f32),
            pltpu.VMEM((YN, ZL, 8, 128), f32),
            pltpu.VMEM((YN, ZL, 8, 128), f32),
            pltpu.VMEM((ZL, 8, 128), f32),
            pltpu.VMEM((ZL * GAS, 8, 128), f32),
            pltpu.VMEM((7, 3 * NXL, 3 * NYL, 128), f32),
            DMA((8,)), DMA((8,)),
            DMA((ZL * GAS - 1,)), DMA((ZL * GAS - 1,)),
            DMA((YN - 1,)), DMA((YN - 1,)),
            DMA((XC - 1,)), DMA((XC - 1,)),
        ],
        compiler_params=pltpu.CompilerParams(collective_id=1, has_side_effects=True),
        name="finish_step",
    )(
        part.reshape(YN, ZL, XC, 8, 128), field_in, flow, density,
        star_pos, star_vel, star_accel, act,
    )
    return (star_new, flow, field_out)


def solution(mesh):
    placed = (
        P(None, ("star", "gas")),
        P(None, ("star", "gas")),
        P(None, ("star", "gas")),
        P(("star", "gas")),
        P(),
        P("star", "gas", None),
        P(None, "star", "gas", None),
        P(None, "star", "gas", None),
    )
    return jax.shard_map(
        body,
        mesh=mesh,
        in_specs=placed,
        out_specs=(
            P(None, ("star", "gas")),
            P(None, "star", "gas", None),
            P(None, "star", "gas", None),
        ),
        check_vma=False,
    )
```

time: 1060 us -> 105 us (0.10)
  blocking collectives: 612 us -> 0 us
  waiting for transfers between devices: 257 us -> 0 us
  other arithmetic: 139 us -> 0 us
  Pallas kernels: 0 us -> 97.8 us
  starting transfers between devices: 16.3 us -> 0 us
  between operations: 14.4 us -> 0.7 us
    all_gather x1 -> x0, blocking collectives: 612 us -> none  [body(): targets = lax.all_gather(packed, ('star', 'gas'), axis=1, tiled=True)]
    psum x1 -> x0, waiting for transfers between devices: 251 us -> none  [body(): summed = lax.psum(partial_terms, ('star', 'gas'))]
    reduce_sum x385 -> x0, other arithmetic: 111 us -> none  [the longest x96 48.2 us: pair_terms(): gas_acc = jnp.sum((inv_cube * cell_mass[None, :])[None] * cell_gap, 2)]
    pallas_call x0 -> x3, Pallas kernels: none -> 97.8 us  [the longest x1 48 us: body(): pl.pallas_call(compute_kernel, out_shape=(jax.ShapeDtypeStruct((TILES, 8,...]
    mul x290 -> x0, other arithmetic: 20 us -> none  [the longest x96 14.6 us: pair_terms(): cell_kick = -jnp.sum((inv_cube * target[6][:, None])[None] * cell_gap, 1)]
    ppermute x8 -> x0, starting transfers between devices: 16.3 us -> none  [the longest x4 14.3 us: with_halo(): lax.ppermute(lax.slice_in_dim(block, 0, width, axis=dim), axis, backward)]
  transfers between devices with their start and end apart: 9 -> 0, of which waited for: 5 -> 0; matrix products, arithmetic and copies ran while one was open for 0% -> 0% of each run, Pallas kernels for 0% -> 0%
where the time goes in v1:
time: 105 us; the launch traced here: 104 us
  Pallas kernels  97.8 us (93%)
  local copies, waits for them, and re-layouts  5.85 us (6%)
    pallas_call x1, Pallas kernels, body(): pl.pallas_call(compute_kernel, out_shape=(jax.ShapeDtypeStruct((TILES, 8,...  48 us
    pallas_call x1, Pallas kernels, body(): pl.pallas_call(finish_kernel, out_shape=(jax.ShapeDtypeStruct((12, STARS)...  27.7 us
    pallas_call x1, Pallas kernels, body(): pl.pallas_call(gather_kernel, out_shape=(jax.ShapeDtypeStruct((YN, ZL, XC...  22.1 us
    unnamed x18, local copies, waits for them, and re-layouts  5.85 us

profile of v1, /device:TPU:32, one launch (start us, length us, event | category | flops | bytes accessed | tf_op | source)
XLA Modules:
  0.0 104.4 jit_solution(11062261107844157953)
XLA Ops:
  0.6 0.0 copy-start.2
  0.6 0.0 copy-start.3
  0.7 22.1 %gather_targets.1 = (f32[4,2,8,8,128]{4,3,2,1,0:T(8,128)}, f32[8,512]{1,0:T(8,128)}, s32[2,128]{1,0:T(2,128)}) custom-call(f32[3,512]{1,0:T(4,128)} %pos.3, f32[3,512]{1,0:T(4,128)} %vel.3, f32[6,512]{1,0:T(8,128)} %accel.3, f32[1,512]{1,0:T(1,128)} %bitcast.9, s32[16,128]{1,0:T(8,128)} %bitcast.6), custom_call_target="tpu_custom_call" | custom-call | tf_op jit(solution)/shard_map/gather_targets/pallas_call | solution.py:471
  22.8 0.0 copy-start.6
  22.8 0.0 copy-done.2
  22.8 0.0 copy-done.3
  22.8 0.6 copy-done.6
  23.5 0.0 copy-start.1
  23.5 0.9 copy-done.1
  24.4 0.0 copy-start.4
  24.4 0.8 copy-done.4
  25.2 0.0 copy-start.5
  25.2 0.7 copy-done.5
  25.9 48.0 %pair_sums.1 = (f32[64,8,128]{2,1,0:T(8,128)S(1)}, f32[3,4,8,64]{3,2,1,0:T(8,128)}) custom-call(f32[64,8,128]{2,1,0:T(8,128)S(1)} %bitcast.5, f32[8,512]{1,0:T(8,128)S(1)} %copy-done.5, s32[2,128]{1,0:T(2,128)S(1)} %copy-done.6, s32[16,128]{1,0:T(8,128)S(1)} %bitcast.8, f32[4,8,64]{2,1,0:T(8,128)S(1)} %copy-done.3, f32[3,4,8,64]{3,2,1,0:T(8,128)S(1)} %copy-done.4), custom_call_target="tpu_custom_call" | custom-call | tf_op jit(solution)/shard_map/pair_sums/pallas_call | solution.py:490
  73.9 0.0 copy-start
  73.9 0.7 copy-done
  74.7 27.7 %finish_step.1 = (f32[12,512]{1,0:T(8,128)}, f32[3,4,8,64]{3,2,1,0:T(8,128)}) custom-call(f32[4,2,8,8,128]{4,3,2,1,0:T(8,128)} %bitcast.4, f32[3,4,8,64]{3,2,1,0:T(8,128)} %field.1, f32[3,4,8,64]{3,2,1,0:T(8,128)} %get-tuple-element.21.flow, f32[4,8,64]{2,1,0:T(8,128)} %density.3, f32[3,512]{1,0:T(4,128)} %pos.3, f32[3,512]{1,0:T(4,128)} %vel.3, ...), custom_call_target="tpu_custom_call" | custom-call | tf_op jit(solution)/shard_map/finish_step/pallas_call | solution.py:513
  102.4 0.0 copy-start.7
  102.4 1.4 %copy.13 = f32[12,512]{1,0:T(8,128)} copy(f32[12,512]{1,0:T(8,128)} %get-tuple-element.20) | data formatting | bytes 49152
  103.8 0.0 copy-done.7
  103.8 0.6 copy.14
Async XLA Ops:
  0.6 22.2 %copy-start.2 = (s32[2048]{0:T(1024)S(1)}, s32[2048]{0:T(1024)}, u32[]{:S(2)}) copy-start(s32[2048]{0:T(1024)} %param.12) | copy-start | bytes 24580
  0.6 22.2 %copy-start.3 = (f32[4,8,64]{2,1,0:T(8,128)S(1)}, f32[4,8,64]{2,1,0:T(8,128)}, u32[]{:S(2)}) copy-start(f32[4,8,64]{2,1,0:T(8,128)} %density.3) | copy-start | bytes 24580
  22.8 0.7 copy-start.6
  23.5 0.9 copy-start.1
  24.4 0.8 copy-start.4
  25.2 0.7 copy-start.5
  73.9 0.7 copy-start
  102.4 1.4 %copy-start.7 = (f32[3,4,8,64]{3,2,1,0:T(8,128)S(1)}, f32[3,4,8,64]{3,2,1,0:T(8,128)}, u32[]{:S(2)}) copy-start(f32[3,4,8,64]{3,2,1,0:T(8,128)} %get-tuple-element.22) | copy-start | bytes 73732

commit v2 on v1

--- a/solution.py
+++ b/solution.py
@@ -21,8 +21,12 @@
 SLOTS = 32
 MOST = 24
 NXL, NYL, NZ = 4, 8, 64
-COLS = NXL * NYL
+WIDE = 256
+WIDES = ACTIVE // WIDE
+CELL_TILES = NXL * NYL * NZ // WIDE
+MIDDLE = 16.0
 f32 = jnp.float32
+bf16 = jnp.bfloat16
 i32 = jnp.int32
 
 
@@ -171,9 +175,36 @@
         copy.wait()
 
 
+def split(v):
+    hi = v.astype(bf16)
+    return hi, (v - hi.astype(f32)).astype(bf16)
+
+
+def twice(v):
+    return jnp.concatenate([v, v], axis=1)
+
+
+def both(v):
+    hi = v.astype(bf16).astype(f32)
+    return jnp.concatenate([hi, v - hi], axis=0).astype(bf16)
+
+
+def dot_nn(lhs, rhs):
+    return jnp.dot(lhs, rhs, preferred_element_type=f32)
+
+
+def dot_nt(lhs, rhs):
+    return lax.dot_general(lhs, rhs, (((1,), (1,)), ((), ())), preferred_element_type=f32)
+
+
+def fold(v):
+    v = v[0:8] + v[8:16]
+    return v[:, 0:WIDE] + v[:, WIDE:] if v.shape[1] > WIDE else v
+
+
 def compute_kernel(
-    tiles, res, begins, active, density, flow_in, part, flow,
-    targ, rb, mb, dz, dz2, mdz, gacc, pt, ks, square
+    tiles, res, begins, active, density, flow_in, begin_of, active_of, part, flow,
+    targ, rb, sm, cm, tm, dz2, mom, kacc, pt, rows8, square, wa, wb, pa, pb
 ):
     star, gas, y, zl, xc = place()
     lane8 = lanes()
@@ -189,13 +220,15 @@
         slot = b * 128 + lane8 - begin
         lane = (owner & (GAS - 1)) * SLOTS + slot
         tile = owner >> 2
+        low, high = active_of[b, 0] >> 11, active_of[b, 127] >> 11
 
         def pick(q, found):
-            for r in range(8):
-                found = jnp.where(tile == q * 8 + r, take_lanes(tiles[q * 8 + r], lane), found)
+            for r in range(4):
+                at = jnp.minimum(low + q * 4 + r, TILES - 1)
+                found = jnp.where(tile == at, take_lanes(tiles[at], lane), found)
             return found
 
-        targ[b] = lax.fori_loop(0, TILES // 8, pick, jnp.zeros((8, 128), f32))
+        targ[b] = lax.fori_loop(0, (high - low) // 4 + 1, pick, jnp.zeros((8, 128), f32))
         return 0
 
     lax.fori_loop(0, BLOCKS, compact, 0)
@@ -204,121 +237,178 @@
     for q in range(STARS // 128):
         square[0:8, :] = res[:, q * 128 : (q + 1) * 128]
         turned = jnp.transpose(square[...])
-        for f in range(7):
-            column = turned[:, f : f + 1]
-            if f == 6:
-                column = column * gravity
-            rb[f, q * 128 : (q + 1) * 128, :] = jnp.broadcast_to(column, (128, 128))
+        for f in range(6):
+            rb[f, q * 128 : (q + 1) * 128, :] = jnp.broadcast_to(turned[:, f : f + 1], (128, 128))
+    gm = res[6:7, :] * gravity
+    rows8[0:1, :] = gm
+    rows8[1:4, :] = gm * (res[0:3, :] - MIDDLE)
+    rows8[4:7, :] = gm * res[3:6, :]
+    rows8[7:8, :] = jnp.zeros((1, STARS), f32)
+    sm[...] = both(rows8[...])
+
+    x_mid = (star * NXL).astype(f32) + 0.5 * NXL
+    y_mid = (gas * NYL).astype(f32) + 0.5 * NYL
+    z_mid = 0.5 * NZ
+    lane1 = lanes((1, 128))
+    z_off = (lane1 & (NZ - 1)).astype(f32) + (0.5 - z_mid)
+    rows8[4:8, :] = jnp.zeros((4, STARS), f32)
     for i in range(NXL):
-        square[i * NYL : (i + 1) * NYL, 0:NZ] = density[i]
-    turned = jnp.transpose(square[...])
-    for c in range(COLS):
-        mb[c] = jnp.broadcast_to(turned[0:NZ, c : c + 1] * gravity, (NZ, 128)).reshape(8, 8, 128)
-
-    def row(b, f):
-        return jnp.broadcast_to(targ[b, f : f + 1, :], (8, 128))
-
-    height = (
-        lax.broadcasted_iota(i32, (8, 8, 128), 0) * 8 + lax.broadcasted_iota(i32, (8, 8, 128), 1)
-    ).astype(f32) + 0.5
-
-    def stars_on(b, _):
-        tx, ty, tz, tu, tv, tw = (row(b, f) for f in range(6))
-
-        def group(g, sums):
-            ax, ay, az, jx, jy, jz = sums
-            for r in range(4):
-                at = pl.ds(pl.multiple_of(g * 32 + r * 8, 8), 8)
-                dx, dy, dzz = rb[0, at, :] - tx, rb[1, at, :] - ty, rb[2, at, :] - tz
-                ux, uy, uz = rb[3, at, :] - tu, rb[4, at, :] - tv, rb[5, at, :] - tw
-                inv = lax.rsqrt(dx * dx + dy * dy + dzz * dzz + soften)
-                inv2 = inv * inv
-                w = rb[6, at, :] * (inv2 * inv)
-                q = 3.0 * (dx * ux + dy * uy + dzz * uz) * inv2
-                ax, ay, az = ax + w * dx, ay + w * dy, az + w * dzz
-                jx = jx + w * (ux - q * dx)
-                jy = jy + w * (uy - q * dy)
-                jz = jz + w * (uz - q * dzz)
-            return ax, ay, az, jx, jy, jz
-
-        zero = jnp.zeros((8, 128), f32)
-        sums = lax.fori_loop(0, STARS // 32, group, (zero,) * 6)
-        for f in range(6):
-            pt[b, f : f + 1, :] = jnp.sum(sums[f], 0, keepdims=True)
-        depth = height - row(b, 2)[None]
-        dz[b] = depth
-        dz2[b] = depth * depth
-        mdz[b] = depth * (row(b, 6) * gravity)[None]
+        cells = twice(density[i]) * gravity
+        for h in range(NYL // 2):
+            q, at = i * 2 + h // 2, (h % 2) * 128
+            cell = jnp.where(lane1 < NZ, cells[2 * h : 2 * h + 1], cells[2 * h + 1 : 2 * h + 2])
+            y_off = jnp.where(lane1 < NZ, 2 * h, 2 * h + 1).astype(f32) + (0.5 - 0.5 * NYL)
+            rows8[0:1, at : at + 128] = cell
+            rows8[1:2, at : at + 128] = cell * (i + 0.5 - 0.5 * NXL)
+            rows8[2:3, at : at + 128] = cell * y_off
+            rows8[3:4, at : at + 128] = cell * z_off
+            if h % 2:
+                cm[q] = both(rows8[:, 0:WIDE])
+
+    def wide(p, f):
+        two = jnp.concatenate([targ[2 * p, f : f + 1, :], targ[2 * p + 1, f : f + 1, :]], axis=1)
+        return jnp.broadcast_to(two, (8, WIDE))
+
+    height = lax.broadcasted_iota(i32, (NZ, WIDE), 0).astype(f32) + 0.5
+
+    def moments(p, _):
+        gm = wide(p, 6)[0:1] * gravity
+        rows8[0:1, 0:WIDE] = gm
+        rows8[1:2, 0:WIDE] = gm * (wide(p, 0)[0:1] - x_mid)
+        rows8[2:3, 0:WIDE] = gm * (wide(p, 1)[0:1] - y_mid)
+        rows8[3:4, 0:WIDE] = gm * (wide(p, 2)[0:1] - z_mid)
+        tm[p] = twice(both(rows8[:, 0:WIDE]))
+        depth = height - jnp.broadcast_to(wide(p, 2)[0:1], (NZ, WIDE))
+        dz2[p] = depth * depth
         for f in range(3):
-            gacc[f, b] = zero
+            mom[f, p] = jnp.zeros((8, WIDE), f32)
         return 0
 
-    lax.fori_loop(0, BLOCKS, stars_on, 0)
-
-    for f in range(3):
-        ks[f] = jnp.zeros((128, 128), f32)
-    x_first = (star * NXL).astype(f32) + 0.5
-    y_first = (gas * NYL).astype(f32) + 0.5
-
-    def column(c, _):
-        x_here = x_first + lax.div(c, NYL).astype(f32)
-        y_here = y_first + lax.rem(c, NYL).astype(f32)
-        cell = mb[c]
-
-        def targets_at(b, sums):
-            kx, ky, kz = sums
-            dx = x_here - row(b, 0)
-            dy = y_here - row(b, 1)
-            tm = row(b, 6) * gravity
-            depth = dz[b]
-            inv = lax.rsqrt((dx * dx + dy * dy + soften)[None] + dz2[b])
-            w = inv * inv * inv
-            u = cell * w
-            total = jnp.sum(u, 0)
-            gacc[0, b] += total * dx
-            gacc[1, b] += total * dy
-            gacc[2, b] += jnp.sum(u * depth, 0)
-            kx = kx + w * (tm * dx)[None]
-            ky = ky + w * (tm * dy)[None]
-            kz = kz + w * mdz[b]
-            return kx, ky, kz
-
-        zero = jnp.zeros((8, 8, 128), f32)
-        sums = lax.fori_loop(0, BLOCKS, targets_at, (zero,) * 3, unroll=2)
-        mark = lanes((NZ, 128)) == c
+    lax.fori_loop(0, WIDES, moments, 0)
+    for buffer in (wa, wb, pa, pb):
+        buffer[...] = jnp.zeros((WIDE, 2 * WIDE), bf16)
+    for q in range(CELL_TILES):
+        kacc[q] = jnp.zeros((8, WIDE), f32)
+
+    def star_weights(p, c, w_buf, p_buf):
+        tx, ty, tz, tu, tv, tw = (jnp.concatenate([wide(p, f)] * 2, axis=0) for f in range(6))
+        for g in range(WIDE // 16):
+            at = pl.ds(c * WIDE + g * 16, 16)
+            dx, dy, dz = twice(rb[0, at, :]) - tx, twice(rb[1, at, :]) - ty, twice(rb[2, at, :]) - tz
+            ux, uy, uz = twice(rb[3, at, :]) - tu, twice(rb[4, at, :]) - tv, twice(rb[5, at, :]) - tw
+            inv = lax.rsqrt(dx * dx + dy * dy + dz * dz + soften)
+            inv2 = inv * inv
+            w = inv2 * inv
+            pull = (dx * ux + dy * uy + dz * uz) * (3.0 * inv2) * w
+            here = slice(g * 16, (g + 1) * 16)
+            w_buf[here, 0:WIDE], w_buf[here, WIDE:] = split(w)
+            p_buf[here, 0:WIDE], p_buf[here, WIDE:] = split(pull)
+
+    def star_sums(p, c, w_buf, p_buf):
+        lhs = sm[:, c * WIDE : (c + 1) * WIDE]
+        mom[0, p] += fold(dot_nn(lhs, w_buf[...]))
+        mom[1, p] += fold(dot_nn(lhs, p_buf[...]))
+
+    def stars_on(p, _):
+        star_sums(jnp.maximum(p - 1, 0), 1, wb, pb)
+        star_weights(p, 0, wa, pa)
+        star_sums(p, 0, wa, pa)
+        star_weights(p, 1, wb, pb)
+        return 0
+
+    lax.fori_loop(0, WIDES, stars_on, 0)
+    star_sums(WIDES - 1, 1, wb, pb)
+    wb[...] = jnp.zeros((WIDE, 2 * WIDE), bf16)
+
+    x_first, y_first = x_mid - 0.5 * NXL + 0.5, y_mid - 0.5 * NYL + 0.5
+
+    def gas_weights(step, half, w_buf):
+        p, i = lax.div(step, NXL), lax.rem(step, NXL)
+        dx = (x_first + i.astype(f32)) - wide(p, 0)
+        dx2 = dx * dx + soften
+        ty = wide(p, 1)
+        for j in range(4):
+            dy = (y_first + (half * 4.0 + j)) - ty
+            side = dx2 + dy * dy
+            side = jnp.concatenate([side, side], axis=0)
+            for g in range(NZ // 16):
+                inv = lax.rsqrt(side + dz2[p, g * 16 : (g + 1) * 16, :])
+                here = slice(j * NZ + g * 16, j * NZ + (g + 1) * 16)
+                w_buf[here, 0:WIDE], w_buf[here, WIDE:] = split(inv * inv * inv)
+
+    def gas_sums(step, half, w_buf):
+        p, i = lax.div(step, NXL), lax.rem(step, NXL)
+        q = i * 2 + half
+        w = w_buf[...]
+        mom[2, p] += fold(dot_nn(cm[q], w))
+        kacc[q] += fold(dot_nt(tm[p], w))
+
+    def gas_on(step, _):
+        gas_sums(jnp.maximum(step - 1, 0), 1, wb)
+        gas_weights(step, 0, wa)
+        gas_sums(step, 0, wa)
+        gas_weights(step, 1, wb)
+        return 0
+
+    lax.fori_loop(0, WIDES * NXL, gas_on, 0)
+    gas_sums(jnp.int32(WIDES * NXL - 1), 1, wb)
+
+    for q in range(CELL_TILES):
+        i, half = q // 2, q % 2
+        sums = kacc[q]
+        for h in range(2):
+            at = slice(h * 128, (h + 1) * 128)
+            y_off = jnp.where(lane1 < NZ, 0, 1).astype(f32) + (half * 4 + h * 2 + 0.5 - 0.5 * NYL)
+            none = sums[0:1, at]
+            kick = (
+                sums[1:2, at] - (i + 0.5 - 0.5 * NXL) * none,
+                sums[2:3, at] - y_off * none,
+                sums[3:4, at] - z_off * none,
+            )
+            for f in range(3):
+                row = jnp.broadcast_to(kick[f], (8, 128))
+                turned = pltpu.roll(row, NZ, 1)
+                j = half * 4 + h * 2
+                flow[f, i, j : j + 1, :] = (
+                    flow_in[f, i, j : j + 1, :] + time_step * row[0:1, 0:NZ]
+                )
+                flow[f, i, j + 1 : j + 2, :] = (
+                    flow_in[f, i, j + 1 : j + 2, :] + time_step * turned[0:1, 0:NZ]
+                )
+
+    def close(p, _):
+        w, pull, g = mom[0, p], mom[1, p], mom[2, p]
+        mids = (x_mid, y_mid, z_mid)
         for f in range(3):
-            column_sum = jnp.sum(sums[f].reshape(NZ, 128), 1, keepdims=True)
-            ks[f, 0:NZ, :] = jnp.where(mark, column_sum, ks[f, 0:NZ, :])
+            at = wide(p, f)[0:1]
+            acc = (w[1 + f : 2 + f] - (at - MIDDLE) * w[0:1]) + (
+                g[1 + f : 2 + f] - (at - mids[f]) * g[0:1]
+            )
+            jerk = (w[4 + f : 5 + f] - wide(p, 3 + f)[0:1] * w[0:1]) - (
+                pull[1 + f : 2 + f] - (at - MIDDLE) * pull[0:1]
+            )
+            for h in range(2):
+                pt[2 * p + h, f : f + 1, :] = acc[:, h * 128 : (h + 1) * 128]
+                pt[2 * p + h, 3 + f : 4 + f, :] = jerk[:, h * 128 : (h + 1) * 128]
+        for h in range(2):
+            pt[2 * p + h, 6:8, :] = jnp.zeros((2, 128), f32)
         return 0
 
-    lax.fori_loop(0, COLS, column, 0)
-    for f in range(3):
-        turned = jnp.transpose(ks[f])
-        for i in range(NXL):
-            flow[f, i] = flow_in[f, i] - time_step * turned[i * NYL : (i + 1) * NYL, 0:NZ]
-
-    def close(b, _):
-        for f in range(3):
-            pt[b, f : f + 1, :] += jnp.sum(gacc[f, b], 0, keepdims=True)
-        pt[b, 6:8, :] = jnp.zeros((2, 128), f32)
-        return 0
-
-    lax.fori_loop(0, BLOCKS, close, 0)
+    lax.fori_loop(0, WIDES, close, 0)
 
     def expand(s, _):
         owner = s * GAS + (lane8 >> 5)
-        begin = jnp.where(
-            owner < 128, take_lanes(begin0, owner & 127), take_lanes(begin1, owner & 127)
-        )
+        begin = jnp.where(s < TILES // 2, take_lanes(begin0, owner & 127), take_lanes(begin1, owner & 127))
         t = jnp.minimum(begin + (lane8 & (SLOTS - 1)), ACTIVE - 1)
         block, lane = t >> 7, t & 127
-        found = jnp.zeros((8, 128), f32)
-        for b in range(BLOCKS):
-            found = jnp.where(block == b, take_lanes(pt[b], lane), found)
-        part[s] = found
+        first = jnp.minimum(begin_of[s // (TILES // 2), (s * GAS) % 128] >> 7, BLOCKS - 1)
+        second = jnp.minimum(first + 1, BLOCKS - 1)
+        part[s] = jnp.where(
+            block == first, take_lanes(pt[first], lane), take_lanes(pt[second], lane)
+        )
         return 0
 
-    lax.fori_loop(0, TILES, expand, 0)
+    lax.fori_loop(0, TILES, expand, 0, unroll=4)
 
 
 def cross_of(lhs, rhs):
@@ -463,6 +553,7 @@
 
 
 VM = pl.BlockSpec(memory_space=pltpu.VMEM)
+SM = pl.BlockSpec(memory_space=pltpu.SMEM)
 DMA = pltpu.SemaphoreType.DMA
 
 
@@ -493,23 +584,28 @@
             jax.ShapeDtypeStruct((TILES, 8, 128), f32),
             jax.ShapeDtypeStruct((3, NXL, NYL, NZ), f32),
         ),
-        in_specs=[VM] * 6,
+        in_specs=[VM] * 6 + [SM] * 2,
         out_specs=(VM,) * 2,
         scratch_shapes=[
             pltpu.VMEM((BLOCKS, 8, 128), f32),
-            pltpu.VMEM((7, STARS, 128), f32),
-            pltpu.VMEM((COLS, 8, 8, 128), f32),
-            pltpu.VMEM((BLOCKS, 8, 8, 128), f32),
-            pltpu.VMEM((BLOCKS, 8, 8, 128), f32),
-            pltpu.VMEM((BLOCKS, 8, 8, 128), f32),
-            pltpu.VMEM((3, BLOCKS, 8, 128), f32),
+            pltpu.VMEM((6, STARS, 128), f32),
+            pltpu.VMEM((16, STARS), bf16),
+            pltpu.VMEM((CELL_TILES, 16, WIDE), bf16),
+            pltpu.VMEM((WIDES, 16, 2 * WIDE), bf16),
+            pltpu.VMEM((WIDES, NZ, WIDE), f32),
+            pltpu.VMEM((3, WIDES, 8, WIDE), f32),
+            pltpu.VMEM((CELL_TILES, 8, WIDE), f32),
             pltpu.VMEM((BLOCKS, 8, 128), f32),
-            pltpu.VMEM((3, 128, 128), f32),
+            pltpu.VMEM((8, STARS), f32),
             pltpu.VMEM((128, 128), f32),
+            pltpu.VMEM((WIDE, 2 * WIDE), bf16),
+            pltpu.VMEM((WIDE, 2 * WIDE), bf16),
+            pltpu.VMEM((WIDE, 2 * WIDE), bf16),
+            pltpu.VMEM((WIDE, 2 * WIDE), bf16),
         ],
         compiler_params=pltpu.CompilerParams(vmem_limit_bytes=48 << 20),
         name="pair_sums",
-    )(tiles.reshape(TILES, 8, 128), res, begins, act, density, flow_in)
+    )(tiles.reshape(TILES, 8, 128), res, begins, act, density, flow_in, begins, act)
     star_new, field_out = pl.pallas_call(
         finish_kernel,
         out_shape=(

time: 105 us -> 83.7 us (0.80)
  Pallas kernels: 97.8 us -> 76.9 us
    pallas_call x1, Pallas kernels: 48 us -> 27.1 us  [body(): pl.pallas_call(compute_kernel, out_shape=(jax.ShapeDtypeStruct((TILES, 8,...]
where the time goes in v2:
time: 83.7 us; the launch traced here: 83.4 us
  Pallas kernels  76.9 us (92%)
  local copies, waits for them, and re-layouts  5.85 us (7%)
    pallas_call x1, Pallas kernels, body(): pl.pallas_call(finish_kernel, out_shape=(jax.ShapeDtypeStruct((12, STARS)...  27.7 us
    pallas_call x1, Pallas kernels, body(): pl.pallas_call(compute_kernel, out_shape=(jax.ShapeDtypeStruct((TILES, 8,...  27.1 us
    pallas_call x1, Pallas kernels, body(): pl.pallas_call(gather_kernel, out_shape=(jax.ShapeDtypeStruct((YN, ZL, XC...  22.1 us
    unnamed x18, local copies, waits for them, and re-layouts  5.85 us

profile of v2, /device:TPU:32, one launch (start us, length us, event | category | flops | bytes accessed | tf_op | source)
XLA Modules:
  0.0 83.4 jit_solution(18376365129816974576)
XLA Ops:
  0.6 0.0 copy-start.2
  0.6 0.0 copy-start.3
  0.7 22.1 %gather_targets.1 = (f32[4,2,8,8,128]{4,3,2,1,0:T(8,128)}, f32[8,512]{1,0:T(8,128)}, s32[2,128]{1,0:T(2,128)}) custom-call(f32[3,512]{1,0:T(4,128)} %pos.3, f32[3,512]{1,0:T(4,128)} %vel.3, f32[6,512]{1,0:T(8,128)} %accel.3, f32[1,512]{1,0:T(1,128)} %bitcast.10, s32[16,128]{1,0:T(8,128)} %bitcast.6), custom_call_target="tpu_custom_call" | custom-call | tf_op jit(solution)/shard_map/gather_targets/pallas_call | solution.py:562
  22.8 0.0 copy-start.6
  22.8 0.0 copy-done.2
  22.8 0.0 copy-done.3
  22.8 0.6 copy-done.6
  23.5 0.0 copy-start.1
  23.5 0.9 %copy-done.1 = f32[4,2,8,8,128]{4,3,2,1,0:T(8,128)S(1)} copy-done((f32[4,2,8,8,128]{4,3,2,1,0:T(8,128)S(1)}, f32[4,2,8,8,128]{4,3,2,1,0:T(8,128)}, u32[]{:S(2)}) %copy-start.1) | copy-done | bytes 262168
  24.4 0.0 copy-start.4
  24.4 0.8 copy-done.4
  25.2 0.0 copy-start.5
  25.2 0.7 copy-done.5
  25.9 27.1 %pair_sums.1 = (f32[64,8,128]{2,1,0:T(8,128)S(1)}, f32[3,4,8,64]{3,2,1,0:T(8,128)}) custom-call(f32[64,8,128]{2,1,0:T(8,128)S(1)} %bitcast.5, f32[8,512]{1,0:T(8,128)S(1)} %copy-done.5, s32[2,128]{1,0:T(2,128)S(1)} %copy-done.6, s32[16,128]{1,0:T(8,128)S(1)} %bitcast.8, f32[4,8,64]{2,1,0:T(8,128)S(1)} %copy-done.3, f32[3,4,8,64]{3,2,1,0:T(8,128)S(1)} %copy-done.4, ...), custom_call_target="tpu_custom_call" | custom-call | tf_op jit(solution)/shard_map/pair_sums/pallas_call | solution.py:581
  53.0 0.0 copy-start
  53.0 0.7 copy-done
  53.7 27.7 %finish_step.1 = (f32[12,512]{1,0:T(8,128)}, f32[3,4,8,64]{3,2,1,0:T(8,128)}) custom-call(f32[4,2,8,8,128]{4,3,2,1,0:T(8,128)} %bitcast.4, f32[3,4,8,64]{3,2,1,0:T(8,128)} %field.1, f32[3,4,8,64]{3,2,1,0:T(8,128)} %get-tuple-element.21.flow, f32[4,8,64]{2,1,0:T(8,128)} %density.3, f32[3,512]{1,0:T(4,128)} %pos.3, f32[3,512]{1,0:T(4,128)} %vel.3, ...), custom_call_target="tpu_custom_call" | custom-call | tf_op jit(solution)/shard_map/finish_step/pallas_call | solution.py:609
  81.4 0.0 copy-start.7
  81.4 1.4 %copy.13 = f32[12,512]{1,0:T(8,128)} copy(f32[12,512]{1,0:T(8,128)} %get-tuple-element.20) | data formatting | bytes 49152
  82.8 0.0 copy-done.7
  82.8 0.6 copy.14
Async XLA Ops:
  0.6 22.2 %copy-start.2 = (s32[2048]{0:T(1024)S(1)}, s32[2048]{0:T(1024)}, u32[]{:S(2)}) copy-start(s32[2048]{0:T(1024)} %param.12) | copy-start | bytes 24580
  0.6 22.2 %copy-start.3 = (f32[4,8,64]{2,1,0:T(8,128)S(1)}, f32[4,8,64]{2,1,0:T(8,128)}, u32[]{:S(2)}) copy-start(f32[4,8,64]{2,1,0:T(8,128)} %density.3) | copy-start | bytes 24580
  22.8 0.7 copy-start.6
  23.5 0.9 %copy-start.1 = (f32[4,2,8,8,128]{4,3,2,1,0:T(8,128)S(1)}, f32[4,2,8,8,128]{4,3,2,1,0:T(8,128)}, u32[]{:S(2)}) copy-start(f32[4,2,8,8,128]{4,3,2,1,0:T(8,128)} %get-tuple-element.10) | copy-start | bytes 786436
  24.4 0.8 copy-start.4
  25.2 0.7 copy-start.5
  53.0 0.7 copy-start
  81.4 1.4 %copy-start.7 = (f32[3,4,8,64]{3,2,1,0:T(8,128)S(1)}, f32[3,4,8,64]{3,2,1,0:T(8,128)}, u32[]{:S(2)}) copy-start(f32[3,4,8,64]{3,2,1,0:T(8,128)} %get-tuple-element.22) | copy-start | bytes 73732

commit v3 on v2

v3 whole, which is shorter than its diff:
```python
import functools

import jax
import jax.numpy as jnp
from jax import lax
from jax.experimental import pallas as pl
from jax.experimental.pallas import tpu as pltpu
from jax.sharding import PartitionSpec as P

MESH = pl.DeviceIdType.MESH
gravity = 0.02
soften = 4.0
time_step = 1.5
field_step = 0.1

STARS = 512
ACTIVE = 2048
BLOCKS = ACTIVE // 128
XC, ZL, YN, GAS = 8, 2, 4, 4
TILES = YN * ZL * XC
PATH = TILES + BLOCKS
SLOTS = 32
MOST = 24
NXL, NYL, NZ = 4, 8, 64
WIDE = 256
WIDES = ACTIVE // WIDE
CELL_TILES = NXL * NYL * NZ // WIDE
MIDDLE = 16.0
f32 = jnp.float32
bf16 = jnp.bfloat16
i32 = jnp.int32


def lanes(shape=(8, 128)):
    return lax.broadcasted_iota(i32, shape, len(shape) - 1)


def take_lanes(values, index):
    return jnp.take_along_axis(values, index, axis=1, mode="promise_in_bounds")


def place():
    star = lax.axis_index("star")
    gas = lax.axis_index("gas")
    xc = lax.rem(star, XC)
    zl = lax.rem(lax.div(star, XC), ZL)
    y = lax.div(star, XC * ZL)
    return star, gas, y, zl, xc


def tile_at(tile):
    return tile >> 4, (tile >> 3) & 1, tile & 7


def star_of(y, zl, xc):
    return (y * ZL + zl) * XC + xc


def z_peers(y, zl, xc, gas):
    zi = zl * GAS + gas
    peers = []
    for d in range(1, ZL * GAS):
        other = lax.rem(zi + d, ZL * GAS)
        ozl, ogas = lax.div(other, GAS), lax.rem(other, GAS)
        peers.append((other, ozl, (star_of(y, ozl, xc), ogas)))
    return zi, peers


def y_peers(y, zl, xc, gas):
    peers = []
    for d in range(1, YN):
        other = lax.rem(y + d, YN)
        peers.append((other, (star_of(other, zl, xc), gas)))
    return peers


def xc_peers(y, zl, xc, gas):
    peers = []
    for d in range(1, XC):
        other = lax.rem(xc + d, XC)
        peers.append((other, (star_of(y, zl, other), gas)))
    return peers


def meet(devices):
    barrier = pltpu.get_barrier_semaphore()
    for device in devices:
        pl.semaphore_signal(barrier, inc=1, device_id=device, device_id_type=MESH)
    return lambda: pl.semaphore_wait(barrier, len(devices))


def send(src, dst, send_sem, recv_sem, device):
    copy = pltpu.make_async_remote_copy(
        src_ref=src, dst_ref=dst, send_sem=send_sem, recv_sem=recv_sem,
        device_id=device, device_id_type=MESH,
    )
    copy.start()
    return copy


def own_indices(active_ref, rank, lane0):
    act = active_ref[...]
    base = rank * STARS
    begin = jnp.sum((act < base).astype(f32)).astype(i32)
    slot = lanes() - lane0
    t = begin + slot
    inside = (slot >= 0) & (slot < SLOTS) & (t < ACTIVE)
    t = jnp.where(inside, t, 0)
    block, lane = t >> 7, t & 127
    found = jnp.full((8, 128), -1, i32)
    for b in range(BLOCKS):
        row = jnp.broadcast_to(active_ref[b : b + 1, :], (8, 128))
        found = jnp.where(block == b, take_lanes(row, lane), found)
    local = found - base
    used = inside & (local >= 0) & (local < STARS)
    return jnp.where(used, local, -1), used


def split(v):
    hi = v.astype(bf16)
    return hi, (v - hi.astype(f32)).astype(bf16)


def twice(v):
    return jnp.concatenate([v, v], axis=1)


def both(v):
    hi = v.astype(bf16).astype(f32)
    return jnp.concatenate([hi, v - hi], axis=0).astype(bf16)


def dot_nn(lhs, rhs):
    return jnp.dot(lhs, rhs, preferred_element_type=f32)


def dot_nt(lhs, rhs):
    return lax.dot_general(lhs, rhs, (((1,), (1,)), ((), ())), preferred_element_type=f32)


def fold(v):
    v = v[0:8] + v[8:16]
    return v[:, 0:WIDE] + v[:, WIDE:] if v.shape[1] > WIDE else v


def cross_of(lhs, rhs):
    return (
        lhs[1] * rhs[2] - lhs[2] * rhs[1],
        lhs[2] * rhs[0] - lhs[0] * rhs[2],
        lhs[0] * rhs[1] - lhs[1] * rhs[0],
    )


def diff_x(v):
    return 0.5 * (v[2:] - v[:-2])


def diff_y(v):
    n = v.shape[1]
    return (0.5 * (pltpu.roll(v, n - 1, 1) - pltpu.roll(v, 1, 1)))[1:-1]


def diff_z(v):
    n = v.shape[2]
    return (0.5 * (pltpu.roll(v, n - 1, 2) - pltpu.roll(v, 1, 2)))[1:-1]


def curl_of(a, b, c):
    return (diff_y(c) - diff_z(b), diff_z(a) - diff_x(c), diff_x(b) - diff_y(a))


def rate_of(field, flow, resist):
    current = curl_of(*field)
    inner = tuple(v[1:-1] for v in field)
    drift = cross_of(cross_of(current, inner), inner)
    motion = cross_of(flow, inner)
    emf = tuple(m + resist * d for m, d in zip(motion, drift))
    return curl_of(*emf)


def step_kernel(
    pos_in, vel_in, accel_in, mass_in, active_in, density_in, flow_from, field_in,
    star_new, flow, field_out,
    pos, vel, accel, mass, active, brick, flow_in, res, own, zbuf, tiles, table, table_of,
    spots, homes, seen, targ, rb, sm, cm, tm, dz2, mom, kacc, pt, rows8, square, wa, wb, pa, pb,
    part, near, wind_near, r1, q1, r2, t2, r3, big,
    ins, zs, zr, ys, yr, xs, xr, hs, hr, fs, fr, zs2, zr2, ys2, yr2, xs2, xr2
):
    star, gas, y, zl, xc = place()
    loads = [
        pltpu.make_async_copy(src, dst, ins.at[n])
        for n, (src, dst) in enumerate((
            (pos_in, pos), (vel_in, vel), (accel_in, accel), (mass_in, mass), (active_in, active),
            (density_in, brick.at[3]), (field_in, brick.at[pl.ds(0, 3)]), (flow_from, flow_in),
        ))
    ]
    for load in loads:
        load.start()
    zi, zp = z_peers(y, zl, xc, gas)
    yp = y_peers(y, zl, xc, gas)
    xp = xc_peers(y, zl, xc, gas)
    sides = []
    for dx in (-1, 0, 1):
        for dy in (-1, 0, 1):
            if dx or dy:
                device = (lax.rem(star + dx + TILES, TILES), lax.rem(gas + dy + GAS, GAS))
                sides.append((dx, dy, device))
    arrived = meet(
        [p[-1] for p in zp] + [p[-1] for p in yp] + [p[-1] for p in xp] + [p[-1] for p in sides]
    )
    for load in loads[:5]:
        load.wait()
    old_acc, old_jerk = accel[0:3, :], accel[3:6, :]
    v = vel[...]
    res[0:3, :] = (
        pos[...] + time_step * v + time_step**2 / 2.0 * old_acc + time_step**3 / 6.0 * old_jerk
    )
    res[3:6, :] = v + time_step * old_acc + time_step**2 / 2.0 * old_jerk
    res[6:7, :] = mass[...]
    res[7:8, :] = jnp.zeros((1, STARS), f32)
    local, used = own_indices(active, star * GAS + gas, gas * SLOTS)
    block, lane = local >> 7, local & 127
    packed = jnp.zeros((8, 128), f32)
    for b in range(STARS // 128):
        packed = jnp.where(
            used & (block == b), take_lanes(res[:, b * 128 : (b + 1) * 128], lane), packed
        )
    own[...] = packed
    zbuf[zi] = packed
    arrived()
    zc = [
        send(own, zbuf.at[zi], zs.at[d], zr.at[d], device)
        for d, (other, ozl, device) in enumerate(zp)
    ]

    lane8 = lanes()
    edge0 = (lanes((128, 128)) * STARS).astype(f32)
    edge1 = edge0 + 128.0 * STARS
    count0 = jnp.zeros((8, 128), f32)
    count1 = jnp.zeros((8, 128), f32)
    for b in range(BLOCKS):
        row = jnp.broadcast_to(active[b : b + 1, :].astype(f32), (128, 128))
        col = jnp.transpose(row)
        less0 = jnp.where(col < edge0, 1.0, 0.0).reshape(16, 8, 128)
        less1 = jnp.where(col < edge1, 1.0, 0.0).reshape(16, 8, 128)
        count0 = count0 + jnp.sum(less0, 0)
        count1 = count1 + jnp.sum(less1, 0)
    begin0 = jnp.broadcast_to(jnp.sum(count0, 0, keepdims=True).astype(i32), (8, 128))
    begin1 = jnp.broadcast_to(jnp.sum(count1, 0, keepdims=True).astype(i32), (8, 128))
    steps = jnp.zeros((8, 128), f32)
    for half, begin in enumerate((begin0, begin1)):
        owner = lane8 + half * 128
        leaves = (owner >> 2) - 1 + (begin >> 7)
        leaves = jnp.where(((owner & 3) == 0) & (owner > 0), leaves, 1000).astype(f32)
        col = jnp.transpose(jnp.broadcast_to(leaves[0:1], (128, 128)))
        past = jnp.where(col < lanes((128, 128)).astype(f32), 1.0, 0.0).reshape(16, 8, 128)
        steps = steps + jnp.sum(past, 0)
    table[0:1, :] = begin0[0:1]
    table[1:2, :] = begin1[0:1]
    tile_of = jnp.sum(steps, 0, keepdims=True)
    table[2:3, :] = tile_of.astype(i32)
    in_block = lanes((1, 128)).astype(f32) - tile_of
    in_block = jnp.where(lanes((1, 128)) < PATH, in_block, 1000.0)
    col = jnp.transpose(jnp.broadcast_to(in_block, (128, 128)))
    past = jnp.where(col <= lanes((128, 128)).astype(f32), 1.0, 0.0).reshape(16, 8, 128)
    last = jnp.sum(jnp.sum(past, 0), 0, keepdims=True) - 1.0
    table[3:4, :] = last.astype(i32)
    table[4:8, :] = jnp.zeros((4, 128), i32)
    to_scalars = pltpu.make_async_copy(table, table_of, ins.at[8])
    to_scalars.start()
    for b in range(BLOCKS):
        act = jnp.broadcast_to(active[b : b + 1, :], (8, 128))
        owner = act >> 9
        begin = jnp.where(
            owner < 128, take_lanes(begin0, owner & 127), take_lanes(begin1, owner & 127)
        )
        spots[b] = ((owner & (GAS - 1)) * SLOTS + b * 128 + lane8 - begin) & 127
        homes[b] = owner >> 2
    to_scalars.wait()
    for copy in zc:
        copy.wait()
    for z in range(ZL):
        merged = zbuf[z * GAS]
        for g in range(1, GAS):
            merged = merged + zbuf[z * GAS + g]
        tiles[y, z, xc] = merged
    yc = [
        send(tiles.at[y, :, xc], tiles.at[y, :, xc], ys.at[d], yr.at[d], device)
        for d, (other, device) in enumerate(yp)
    ]
    square[...] = jnp.zeros((128, 128), f32)
    for q in range(STARS // 128):
        square[0:8, :] = res[:, q * 128 : (q + 1) * 128]
        turned = jnp.transpose(square[...])
        for f in range(6):
            rb[f, q * 128 : (q + 1) * 128, :] = jnp.broadcast_to(turned[:, f : f + 1], (128, 128))
    gm = res[6:7, :] * gravity
    rows8[0:1, :] = gm
    rows8[1:4, :] = gm * (res[0:3, :] - MIDDLE)
    rows8[4:7, :] = gm * res[3:6, :]
    rows8[7:8, :] = jnp.zeros((1, STARS), f32)
    sm[...] = both(rows8[...])

    for copy in yc:
        copy.wait()
    xcs = [
        send(tiles.at[:, :, xc], tiles.at[:, :, xc], xs.at[d], xr.at[d], device)
        for d, (other, device) in enumerate(xp)
    ]
    for load in loads[5:]:
        load.wait()
    x_mid = (star * NXL).astype(f32) + 0.5 * NXL
    y_mid = (gas * NYL).astype(f32) + 0.5 * NYL
    z_mid = 0.5 * NZ
    lane1 = lanes((1, 128))
    z_off = (lane1 & (NZ - 1)).astype(f32) + (0.5 - z_mid)
    rows8[4:8, :] = jnp.zeros((4, STARS), f32)
    for i in range(NXL):
        cells = twice(brick[3, i]) * gravity
        for h in range(NYL // 2):
            q, at = i * 2 + h // 2, (h % 2) * 128
            cell = jnp.where(lane1 < NZ, cells[2 * h : 2 * h + 1], cells[2 * h + 1 : 2 * h + 2])
            y_off = jnp.where(lane1 < NZ, 2 * h, 2 * h + 1).astype(f32) + (0.5 - 0.5 * NYL)
            rows8[0:1, at : at + 128] = cell
            rows8[1:2, at : at + 128] = cell * (i + 0.5 - 0.5 * NXL)
            rows8[2:3, at : at + 128] = cell * y_off
            rows8[3:4, at : at + 128] = cell * z_off
            if h % 2:
                cm[q] = both(rows8[:, 0:WIDE])

    for buffer in (wa, wb, pa, pb):
        buffer[...] = jnp.zeros((WIDE, 2 * WIDE), bf16)
    for q in range(CELL_TILES):
        kacc[q] = jnp.zeros((8, WIDE), f32)
    for copy in xcs:
        copy.wait()
    hcs = [
        send(brick, near.at[1 - dx, 1 - dy], hs.at[d], hr.at[d], device)
        for d, (dx, dy, device) in enumerate(sides)
    ]
    near[1, 1] = brick[...]

    def walk(n, now):
        for r in range(8):
            step = n * 8 + r
            tile = jnp.clip(table_of[2, step], 0, TILES - 1)
            at = jnp.clip(step - tile, 0, BLOCKS - 1)
            ty, tz, tx = tile_at(tile)
            values = take_lanes(tiles[ty, tz, tx], spots[at])
            now = jnp.where(homes[at] == tile, values, now)
            seen[step] = now
        return now

    lax.fori_loop(0, PATH // 8, walk, jnp.zeros((8, 128), f32))
    for b in range(BLOCKS):
        targ[b] = seen[jnp.clip(table_of[3, b], 0, PATH - 1)]

    def wide(p, f):
        two = jnp.concatenate([targ[2 * p, f : f + 1, :], targ[2 * p + 1, f : f + 1, :]], axis=1)
        return jnp.broadcast_to(two, (8, WIDE))

    height = lax.broadcasted_iota(i32, (NZ, WIDE), 0).astype(f32) + 0.5

    def moments(p, _):
        gm = wide(p, 6)[0:1] * gravity
        rows8[0:1, 0:WIDE] = gm
        rows8[1:2, 0:WIDE] = gm * (wide(p, 0)[0:1] - x_mid)
        rows8[2:3, 0:WIDE] = gm * (wide(p, 1)[0:1] - y_mid)
        rows8[3:4, 0:WIDE] = gm * (wide(p, 2)[0:1] - z_mid)
        tm[p] = twice(both(rows8[:, 0:WIDE]))
        depth = height - jnp.broadcast_to(wide(p, 2)[0:1], (NZ, WIDE))
        dz2[p] = depth * depth
        for f in range(3):
            mom[f, p] = jnp.zeros((8, WIDE), f32)
        return 0

    lax.fori_loop(0, WIDES, moments, 0)

    x_first, y_first = x_mid - 0.5 * NXL + 0.5, y_mid - 0.5 * NYL + 0.5

    def gas_weights(step, half, w_buf):
        p, i = lax.div(step, NXL), lax.rem(step, NXL)
        dx = (x_first + i.astype(f32)) - wide(p, 0)
        dx2 = dx * dx + soften
        ty = wide(p, 1)
        for j in range(4):
            dy = (y_first + (half * 4.0 + j)) - ty
            side = dx2 + dy * dy
            side = jnp.concatenate([side, side], axis=0)
            for g in range(NZ // 16):
                inv = lax.rsqrt(side + dz2[p, g * 16 : (g + 1) * 16, :])
                here = slice(j * NZ + g * 16, j * NZ + (g + 1) * 16)
                w_buf[here, 0:WIDE], w_buf[here, WIDE:] = split(inv * inv * inv)

    def gas_sums(step, half, w_buf):
        p, i = lax.div(step, NXL), lax.rem(step, NXL)
        q = i * 2 + half
        w = w_buf[...]
        mom[2, p] += fold(dot_nn(cm[q], w))
        kacc[q] += fold(dot_nt(tm[p], w))

    def gas_on(step, _):
        gas_sums(jnp.maximum(step - 1, 0), 1, wb)
        gas_weights(step, 0, wa)
        gas_sums(step, 0, wa)
        gas_weights(step, 1, wb)
        return 0

    lax.fori_loop(0, WIDES * NXL, gas_on, 0)
    gas_sums(jnp.int32(WIDES * NXL - 1), 1, wb)

    for q in range(CELL_TILES):
        i, half = q // 2, q % 2
        sums = kacc[q]
        for h in range(2):
            at = slice(h * 128, (h + 1) * 128)
            y_off = jnp.where(lane1 < NZ, 0, 1).astype(f32) + (half * 4 + h * 2 + 0.5 - 0.5 * NYL)
            none = sums[0:1, at]
            kick = (
                sums[1:2, at] - (i + 0.5 - 0.5 * NXL) * none,
                sums[2:3, at] - y_off * none,
                sums[3:4, at] - z_off * none,
            )
            for f in range(3):
                row = jnp.broadcast_to(kick[f], (8, 128))
                turned = pltpu.roll(row, NZ, 1)
                j = half * 4 + h * 2
                flow[f, i, j : j + 1, :] = (
                    flow_in[f, i, j : j + 1, :] + time_step * row[0:1, 0:NZ]
                )
                flow[f, i, j + 1 : j + 2, :] = (
                    flow_in[f, i, j + 1 : j + 2, :] + time_step * turned[0:1, 0:NZ]
                )

    wind_near[1, 1] = flow[...]
    fcs = [
        send(flow, wind_near.at[1 - dx, 1 - dy], fs.at[d], fr.at[d], device)
        for d, (dx, dy, device) in enumerate(sides)
    ]
    wb[...] = jnp.zeros((WIDE, 2 * WIDE), bf16)

    def star_weights(p, c, w_buf, p_buf):
        tx, ty, tz, tu, tv, tw = (jnp.concatenate([wide(p, f)] * 2, axis=0) for f in range(6))
        for g in range(WIDE // 16):
            at = pl.ds(c * WIDE + g * 16, 16)
            dx, dy, dz = twice(rb[0, at, :]) - tx, twice(rb[1, at, :]) - ty, twice(rb[2, at, :]) - tz
            ux, uy, uz = twice(rb[3, at, :]) - tu, twice(rb[4, at, :]) - tv, twice(rb[5, at, :]) - tw
            inv = lax.rsqrt(dx * dx + dy * dy + dz * dz + soften)
            inv2 = inv * inv
            w = inv2 * inv
            pull = (dx * ux + dy * uy + dz * uz) * (3.0 * inv2) * w
            here = slice(g * 16, (g + 1) * 16)
            w_buf[here, 0:WIDE], w_buf[here, WIDE:] = split(w)
            p_buf[here, 0:WIDE], p_buf[here, WIDE:] = split(pull)

    def star_sums(p, c, w_buf, p_buf):
        lhs = sm[:, c * WIDE : (c + 1) * WIDE]
        mom[0, p] += fold(dot_nn(lhs, w_buf[...]))
        mom[1, p] += fold(dot_nn(lhs, p_buf[...]))

    def stars_on(p, _):
        star_sums(jnp.maximum(p - 1, 0), 1, wb, pb)
        star_weights(p, 0, wa, pa)
        star_sums(p, 0, wa, pa)
        star_weights(p, 1, wb, pb)
        return 0

    lax.fori_loop(0, WIDES, stars_on, 0)
    star_sums(WIDES - 1, 1, wb, pb)
    def close(p, _):
        w, pull, g = mom[0, p], mom[1, p], mom[2, p]
        mids = (x_mid, y_mid, z_mid)
        for f in range(3):
            at = wide(p, f)[0:1]
            acc = (w[1 + f : 2 + f] - (at - MIDDLE) * w[0:1]) + (
                g[1 + f : 2 + f] - (at - mids[f]) * g[0:1]
            )
            jerk = (w[4 + f : 5 + f] - wide(p, 3 + f)[0:1] * w[0:1]) - (
                pull[1 + f : 2 + f] - (at - MIDDLE) * pull[0:1]
            )
            for h in range(2):
                pt[2 * p + h, f : f + 1, :] = acc[:, h * 128 : (h + 1) * 128]
                pt[2 * p + h, 3 + f : 4 + f, :] = jerk[:, h * 128 : (h + 1) * 128]
        for h in range(2):
            pt[2 * p + h, 6:8, :] = jnp.zeros((2, 128), f32)
        return 0

    lax.fori_loop(0, WIDES, close, 0)

    def expand(s, _):
        owner = s * GAS + (lane8 >> 5)
        begin = jnp.where(s < TILES // 2, take_lanes(begin0, owner & 127), take_lanes(begin1, owner & 127))
        t = jnp.minimum(begin + (lane8 & (SLOTS - 1)), ACTIVE - 1)
        block, lane = t >> 7, t & 127
        first = jnp.clip(table_of[s >> 5, (s << 2) & 127] >> 7, 0, BLOCKS - 1)
        second = jnp.minimum(first + 1, BLOCKS - 1)
        ty, tz, tx = tile_at(s)
        part[ty, tz, tx] = jnp.where(
            block == first, take_lanes(pt[first], lane), take_lanes(pt[second], lane)
        )
        return 0

    lax.fori_loop(0, TILES, expand, 0, unroll=4)

    xcs = [
        send(part.at[:, :, other], r1.at[xc], xs2.at[d], xr2.at[d], device)
        for d, (other, device) in enumerate(xp)
    ]
    r1[xc] = part[:, :, xc]

    for copy in hcs:
        copy.wait()
    for copy in fcs:
        copy.wait()
    for c in range(7):
        for dx in range(3):
            for dy in range(3):
                for i in range(NXL):
                    v = near[dx, dy, c, i] if c < 4 else wind_near[dx, dy, c - 4, i]
                    big[c, dx * NXL + i, dy * NYL : (dy + 1) * NYL, :] = twice(v)
    mag = tuple(big[c] for c in range(3))
    wind = tuple(big[4 + c] for c in range(3))
    inv = lax.rsqrt(big[3])
    resist = inv * inv * inv
    first = rate_of(mag, tuple(v[1:-1] for v in wind), resist[1:-1])
    one = tuple(m[2:-2] + field_step * r for m, r in zip(mag, first))
    second = rate_of(one, tuple(v[3:-3] for v in wind), resist[3:-3])
    for c in range(3):
        out = 0.5 * (mag[c][4:-4] + one[c][2:-2] + field_step * second[c])
        field_out[c] = out[:, NYL : 2 * NYL, 0:NZ]

    for copy in xcs:
        copy.wait()
    total = r1[0]
    for n in range(1, XC):
        total = total + r1[n]
    q1[...] = total
    ycs = [
        send(q1.at[other], r2.at[y], ys2.at[d], yr2.at[d], device)
        for d, (other, device) in enumerate(yp)
    ]
    r2[y] = q1[y]
    local, used = own_indices(active, star * GAS + gas, 0)
    for copy in ycs:
        copy.wait()
    total = r2[0]
    for n in range(1, YN):
        total = total + r2[n]
    t2[...] = total
    zcs = [
        send(t2.at[ozl], r3.at[zi], zs2.at[d], zr2.at[d], device)
        for d, (other, ozl, device) in enumerate(zp)
    ]
    r3[zi] = t2[zl]
    for copy in zcs:
        copy.wait()
    total = r3[0]
    for n in range(1, ZL * GAS):
        total = total + r3[n]
    mine = pltpu.roll(total, lax.rem(128 - gas * SLOTS, 128), 1)
    index = lanes((8, STARS))
    sums = jnp.zeros((8, STARS), f32)
    hit = jnp.zeros((8, STARS), f32)
    for s in range(MOST):
        here = index == local[:, s : s + 1]
        sums = jnp.where(here, mine[:, s : s + 1], sums)
        hit = jnp.where(here, 1.0, hit)
    is_active = hit[0:3] > 0.5
    new_acc, new_jerk = sums[0:3], sums[3:6]
    p, v = pos[...], vel[...]
    old_acc, old_jerk = accel[0:3, :], accel[3:6, :]
    vel_one = v + time_step * (old_acc + new_acc) / 2.0 + time_step**2 * (old_jerk - new_jerk) / 12.0
    pos_one = p + time_step * (v + vel_one) / 2.0 + time_step**2 * (old_acc - new_acc) / 12.0
    star_new[0:3, :] = jnp.where(is_active, pos_one, p)
    star_new[3:6, :] = jnp.where(is_active, vel_one, v)
    star_new[6:9, :] = jnp.where(is_active, new_acc, old_acc)
    star_new[9:12, :] = jnp.where(is_active, new_jerk, old_jerk)


VM = pl.BlockSpec(memory_space=pltpu.VMEM)
ANY = pl.BlockSpec(memory_space=pl.ANY)
DMA = pltpu.SemaphoreType.DMA


def body(star_pos, star_vel, star_accel, star_mass, active, density, flow_in, field_in):
    brick = (NXL, NYL, NZ)
    zn = ZL * GAS
    pairs = [DMA((n,)) for n in (zn - 1, zn - 1, YN - 1, YN - 1, XC - 1, XC - 1)]
    star_new, flow, field_out = pl.pallas_call(
        step_kernel,
        out_shape=(
            jax.ShapeDtypeStruct((12, STARS), f32),
            jax.ShapeDtypeStruct((3,) + brick, f32),
            jax.ShapeDtypeStruct((3,) + brick, f32),
        ),
        in_specs=[ANY] * 8,
        out_specs=(VM,) * 3,
        scratch_shapes=[
            pltpu.VMEM((3, STARS), f32),
            pltpu.VMEM((3, STARS), f32),
            pltpu.VMEM((6, STARS), f32),
            pltpu.VMEM((1, STARS), f32),
            pltpu.VMEM((BLOCKS, 128), i32),
            pltpu.VMEM((4,) + brick, f32),
            pltpu.VMEM((3,) + brick, f32),
            pltpu.VMEM((8, STARS), f32),
            pltpu.VMEM((8, 128), f32),
            pltpu.VMEM((zn, 8, 128), f32),
            pltpu.VMEM((YN, ZL, XC, 8, 128), f32),
            pltpu.VMEM((8, 128), i32),
            pltpu.SMEM((8, 128), i32),
            pltpu.VMEM((BLOCKS, 8, 128), i32),
            pltpu.VMEM((BLOCKS, 8, 128), i32),
            pltpu.VMEM((PATH, 8, 128), f32),
            pltpu.VMEM((BLOCKS, 8, 128), f32),
            pltpu.VMEM((6, STARS, 128), f32),
            pltpu.VMEM((16, STARS), bf16),
            pltpu.VMEM((CELL_TILES, 16, WIDE), bf16),
            pltpu.VMEM((WIDES, 16, 2 * WIDE), bf16),
            pltpu.VMEM((WIDES, NZ, WIDE), f32),
            pltpu.VMEM((3, WIDES, 8, WIDE), f32),
            pltpu.VMEM((CELL_TILES, 8, WIDE), f32),
            pltpu.VMEM((BLOCKS, 8, 128), f32),
            pltpu.VMEM((8, STARS), f32),
            pltpu.VMEM((128, 128), f32),
            pltpu.VMEM((WIDE, 2 * WIDE), bf16),
            pltpu.VMEM((WIDE, 2 * WIDE), bf16),
            pltpu.VMEM((WIDE, 2 * WIDE), bf16),
            pltpu.VMEM((WIDE, 2 * WIDE), bf16),
            pltpu.VMEM((YN, ZL, XC, 8, 128), f32),
            pltpu.VMEM((3, 3, 4) + brick, f32),
            pltpu.VMEM((3, 3, 3) + brick, f32),
            pltpu.VMEM((XC, YN, ZL, 8, 128), f32),
            pltpu.VMEM((YN, ZL, 8, 128), f32),
            pltpu.VMEM((YN, ZL, 8, 128), f32),
            pltpu.VMEM((ZL, 8, 128), f32),
            pltpu.VMEM((zn, 8, 128), f32),
            pltpu.VMEM((7, 3 * NXL, 3 * NYL, 128), f32),
            DMA((9,)), *pairs, DMA((8,)), DMA((8,)), DMA((8,)), DMA((8,)), *pairs,
        ],
        compiler_params=pltpu.CompilerParams(
            collective_id=0, has_side_effects=True, vmem_limit_bytes=63 << 20
        ),
        name="block_step",
    )(
        star_pos, star_vel, star_accel, star_mass.reshape(1, STARS),
        active.reshape(BLOCKS, 128), density, flow_in, field_in,
    )
    return (star_new, flow, field_out)


def solution(mesh):
    placed = (
        P(None, ("star", "gas")),
        P(None, ("star", "gas")),
        P(None, ("star", "gas")),
        P(("star", "gas")),
        P(),
        P("star", "gas", None),
        P(None, "star", "gas", None),
        P(None, "star", "gas", None),
    )
    return jax.shard_map(
        body,
        mesh=mesh,
        in_specs=placed,
        out_specs=(
            P(None, ("star", "gas")),
            P(None, "star", "gas", None),
            P(None, "star", "gas", None),
        ),
        check_vma=False,
    )
```

time: 83.7 us -> 64.8 us (0.77)
  Pallas kernels: 76.9 us -> 61.1 us
  local copies, waits for them, and re-layouts: 5.85 us -> 2.83 us
    pallas_call x3 -> x1, Pallas kernels: 76.9 us -> 61.1 us  [body(): pl.pallas_call(step_kernel, out_shape=(jax.ShapeDtypeStruct((12, STARS),...]
    unnamed x18 -> x7, local copies, waits for them, and re-layouts: 5.85 us -> 2.83 us
where the time goes in v3:
time: 64.8 us; the launch traced here: 64.6 us
  Pallas kernels  61.1 us (94%)
  local copies, waits for them, and re-layouts  2.83 us (4%)
  between operations  0.65 us (1%)
    pallas_call x1, Pallas kernels, body(): pl.pallas_call(step_kernel, out_shape=(jax.ShapeDtypeStruct((12, STARS),...  61.1 us
    unnamed x7, local copies, waits for them, and re-layouts  2.83 us

profile of v3, /device:TPU:32, one launch (start us, length us, event | category | flops | bytes accessed | tf_op | source)
XLA Modules:
  0.0 64.6 jit_solution(1744336899160525434)
XLA Ops:
  0.6 61.1 %block_step.1 = (f32[12,512]{1,0:T(8,128)}, f32[3,4,8,64]{3,2,1,0:T(8,128)}, f32[3,4,8,64]{3,2,1,0:T(8,128)}) custom-call(f32[3,512]{1,0:T(4,128)} %pos_in.1, f32[3,512]{1,0:T(4,128)} %vel_in.1, f32[6,512]{1,0:T(8,128)} %accel_in.1, f32[1,512]{1,0:T(1,128)} %bitcast.3, s32[16,128]{1,0:T(8,128)} %bitcast.2, f32[4,8,64]{2,1,0:T(8,128)} %density_in.1, ...), custom_call_target="tpu_custom_call" | custom-call | tf_op jit(solution)/shard_map/block_step/pallas_call | solution.py:589
  61.7 0.0 copy-start.1
  61.7 1.4 %copy.14 = f32[12,512]{1,0:T(8,128)} copy(f32[12,512]{1,0:T(8,128)} %get-tuple-element.6) | data formatting | bytes 49152
  63.1 0.0 copy-done.1
  63.1 0.0 copy-start
  63.1 0.6 copy.15
  63.8 0.2 copy-done
  63.9 0.6 copy.16
Async XLA Ops:
  61.7 1.4 %copy-start.1 = (f32[3,4,8,64]{3,2,1,0:T(8,128)S(1)}, f32[3,4,8,64]{3,2,1,0:T(8,128)}, u32[]{:S(2)}) copy-start(f32[3,4,8,64]{3,2,1,0:T(8,128)} %get-tuple-element.7) | copy-start | bytes 73732
  63.1 0.8 %copy-start = (f32[3,4,8,64]{3,2,1,0:T(8,128)S(1)}, f32[3,4,8,64]{3,2,1,0:T(8,128)}, u32[]{:S(2)}) copy-start(f32[3,4,8,64]{3,2,1,0:T(8,128)} %get-tuple-element.8) | copy-start | bytes 73732

commit v4 on v3

--- a/solution.py
+++ b/solution.py
@@ -16,8 +16,9 @@
 STARS = 512
 ACTIVE = 2048
 BLOCKS = ACTIVE // 128
-XC, ZL, YN, GAS = 8, 2, 4, 4
-TILES = YN * ZL * XC
+XN, CORES, ZL, YN, GAS = 4, 2, 2, 4, 4
+TILES = YN * ZL * XN * CORES
+HALF = TILES // CORES
 PATH = TILES + BLOCKS
 SLOTS = 32
 MOST = 24
@@ -42,44 +43,39 @@
 def place():
     star = lax.axis_index("star")
     gas = lax.axis_index("gas")
-    xc = lax.rem(star, XC)
-    zl = lax.rem(lax.div(star, XC), ZL)
-    y = lax.div(star, XC * ZL)
-    return star, gas, y, zl, xc
-
-
-def tile_at(tile):
-    return tile >> 4, (tile >> 3) & 1, tile & 7
-
-
-def star_of(y, zl, xc):
-    return (y * ZL + zl) * XC + xc
-
-
-def z_peers(y, zl, xc, gas):
+    core = lax.rem(star, CORES)
+    x = lax.rem(lax.div(star, CORES), XN)
+    zl = lax.rem(lax.div(star, CORES * XN), ZL)
+    y = lax.div(star, CORES * XN * ZL)
+    return star, gas, y, zl, x, core
+
+
+def seat(star):
+    return ((star & 1) << 5) | ((star >> 4) << 3) | (((star >> 1) & 3) << 1) | ((star >> 3) & 1)
+
+
+def star_of(y, zl, x, core):
+    return ((y * ZL + zl) * XN + x) * CORES + core
+
+
+def z_peers(y, zl, x, core, gas):
     zi = zl * GAS + gas
     peers = []
     for d in range(1, ZL * GAS):
         other = lax.rem(zi + d, ZL * GAS)
         ozl, ogas = lax.div(other, GAS), lax.rem(other, GAS)
-        peers.append((other, ozl, (star_of(y, ozl, xc), ogas)))
+        peers.append((ozl, (star_of(y, ozl, x, core), ogas)))
     return zi, peers
 
 
-def y_peers(y, zl, xc, gas):
+def plane_peers(y, zl, x, core, gas):
     peers = []
-    for d in range(1, YN):
-        other = lax.rem(y + d, YN)
-        peers.append((other, (star_of(other, zl, xc), gas)))
-    return peers
-
-
-def xc_peers(y, zl, xc, gas):
-    peers = []
-    for d in range(1, XC):
-        other = lax.rem(xc + d, XC)
-        peers.append((other, (star_of(y, zl, other), gas)))
-    return peers
+    for dy in range(YN):
+        for dx in range(XN):
+            if dy or dx:
+                oy, ox = lax.rem(y + dy, YN), lax.rem(x + dx, XN)
+                peers.append((oy * XN + ox, (star_of(oy, zl, ox, core), gas)))
+    return y * XN + x, peers
 
 
 def meet(devices):
@@ -184,9 +180,9 @@
     pos, vel, accel, mass, active, brick, flow_in, res, own, zbuf, tiles, table, table_of,
     spots, homes, seen, targ, rb, sm, cm, tm, dz2, mom, kacc, pt, rows8, square, wa, wb, pa, pb,
     part, near, wind_near, r1, q1, r2, t2, r3, big,
-    ins, zs, zr, ys, yr, xs, xr, hs, hr, fs, fr, zs2, zr2, ys2, yr2, xs2, xr2
+    ins, zs, zr, ps, pr, cs, cr, hs, hr, fs, fr, zs2, zr2, ps2, pr2, cs2, cr2
 ):
-    star, gas, y, zl, xc = place()
+    star, gas, y, zl, x, core = place()
     loads = [
         pltpu.make_async_copy(src, dst, ins.at[n])
         for n, (src, dst) in enumerate((
@@ -196,9 +192,9 @@
     ]
     for load in loads:
         load.start()
-    zi, zp = z_peers(y, zl, xc, gas)
-    yp = y_peers(y, zl, xc, gas)
-    xp = xc_peers(y, zl, xc, gas)
+    zi, zp = z_peers(y, zl, x, core, gas)
+    pi, pp = plane_peers(y, zl, x, core, gas)
+    partner = (star_of(y, zl, x, 1 - core), gas)
     sides = []
     for dx in (-1, 0, 1):
         for dy in (-1, 0, 1):
@@ -206,7 +202,7 @@
                 device = (lax.rem(star + dx + TILES, TILES), lax.rem(gas + dy + GAS, GAS))
                 sides.append((dx, dy, device))
     arrived = meet(
-        [p[-1] for p in zp] + [p[-1] for p in yp] + [p[-1] for p in xp] + [p[-1] for p in sides]
+        [p[-1] for p in zp] + [p[-1] for p in pp] + [p[-1] for p in sides] + [partner]
     )
     for load in loads[:5]:
         load.wait()
@@ -230,7 +226,7 @@
     arrived()
     zc = [
         send(own, zbuf.at[zi], zs.at[d], zr.at[d], device)
-        for d, (other, ozl, device) in enumerate(zp)
+        for d, (ozl, device) in enumerate(zp)
     ]
 
     lane8 = lanes()
@@ -255,17 +251,19 @@
         col = jnp.transpose(jnp.broadcast_to(leaves[0:1], (128, 128)))
         past = jnp.where(col < lanes((128, 128)).astype(f32), 1.0, 0.0).reshape(16, 8, 128)
         steps = steps + jnp.sum(past, 0)
-    table[0:1, :] = begin0[0:1]
-    table[1:2, :] = begin1[0:1]
     tile_of = jnp.sum(steps, 0, keepdims=True)
-    table[2:3, :] = tile_of.astype(i32)
+    whole = jnp.clip(tile_of.astype(i32), 0, TILES - 1)
+    table[0:1, :] = jnp.clip(begin0[0:1] >> 7, 0, BLOCKS - 1)
+    table[1:2, :] = jnp.clip(begin1[0:1] >> 7, 0, BLOCKS - 1)
+    table[2:3, :] = seat(whole)
+    table[3:4, :] = jnp.clip(lanes((1, 128)) - whole, 0, BLOCKS - 1)
     in_block = lanes((1, 128)).astype(f32) - tile_of
     in_block = jnp.where(lanes((1, 128)) < PATH, in_block, 1000.0)
     col = jnp.transpose(jnp.broadcast_to(in_block, (128, 128)))
     past = jnp.where(col <= lanes((128, 128)).astype(f32), 1.0, 0.0).reshape(16, 8, 128)
     last = jnp.sum(jnp.sum(past, 0), 0, keepdims=True) - 1.0
-    table[3:4, :] = last.astype(i32)
-    table[4:8, :] = jnp.zeros((4, 128), i32)
+    table[4:5, :] = jnp.clip(last.astype(i32), 0, PATH - 1)
+    table[5:8, :] = jnp.zeros((3, 128), i32)
     to_scalars = pltpu.make_async_copy(table, table_of, ins.at[8])
     to_scalars.start()
     for b in range(BLOCKS):
@@ -275,18 +273,20 @@
             owner < 128, take_lanes(begin0, owner & 127), take_lanes(begin1, owner & 127)
         )
         spots[b] = ((owner & (GAS - 1)) * SLOTS + b * 128 + lane8 - begin) & 127
-        homes[b] = owner >> 2
+        homes[b] = seat(owner >> 2)
     to_scalars.wait()
     for copy in zc:
         copy.wait()
+    mine_at = core * HALF + pi * ZL
     for z in range(ZL):
         merged = zbuf[z * GAS]
         for g in range(1, GAS):
             merged = merged + zbuf[z * GAS + g]
-        tiles[y, z, xc] = merged
-    yc = [
-        send(tiles.at[y, :, xc], tiles.at[y, :, xc], ys.at[d], yr.at[d], device)
-        for d, (other, device) in enumerate(yp)
+        tiles[mine_at + z] = merged
+    pair = pl.ds(mine_at, ZL)
+    pcs = [
+        send(tiles.at[pair], tiles.at[pair], ps.at[d], pr.at[d], device)
+        for d, (other, device) in enumerate(pp)
     ]
     square[...] = jnp.zeros((128, 128), f32)
     for q in range(STARS // 128):
@@ -301,12 +301,10 @@
     rows8[7:8, :] = jnp.zeros((1, STARS), f32)
     sm[...] = both(rows8[...])
 
-    for copy in yc:
+    for copy in pcs:
         copy.wait()
-    xcs = [
-        send(tiles.at[:, :, xc], tiles.at[:, :, xc], xs.at[d], xr.at[d], device)
-        for d, (other, device) in enumerate(xp)
-    ]
+    half = pl.ds(core * HALF, HALF)
+    cc = send(tiles.at[half], tiles.at[half], cs.at[0], cr.at[0], partner)
     for load in loads[5:]:
         load.wait()
     x_mid = (star * NXL).astype(f32) + 0.5 * NXL
@@ -332,28 +330,21 @@
         buffer[...] = jnp.zeros((WIDE, 2 * WIDE), bf16)
     for q in range(CELL_TILES):
         kacc[q] = jnp.zeros((8, WIDE), f32)
-    for copy in xcs:
-        copy.wait()
+    cc.wait()
     hcs = [
         send(brick, near.at[1 - dx, 1 - dy], hs.at[d], hr.at[d], device)
         for d, (dx, dy, device) in enumerate(sides)
     ]
     near[1, 1] = brick[...]
 
-    def walk(n, now):
-        for r in range(8):
-            step = n * 8 + r
-            tile = jnp.clip(table_of[2, step], 0, TILES - 1)
-            at = jnp.clip(step - tile, 0, BLOCKS - 1)
-            ty, tz, tx = tile_at(tile)
-            values = take_lanes(tiles[ty, tz, tx], spots[at])
-            now = jnp.where(homes[at] == tile, values, now)
-            seen[step] = now
-        return now
-
-    lax.fori_loop(0, PATH // 8, walk, jnp.zeros((8, 128), f32))
+    now = jnp.zeros((8, 128), f32)
+    for step in range(PATH - 1):
+        tile = jnp.clip(table_of[2, step], 0, TILES - 1)
+        at = jnp.clip(table_of[3, step], 0, BLOCKS - 1)
+        now = jnp.where(homes[at] == tile, take_lanes(tiles[tile], spots[at]), now)
+        seen[step] = now
     for b in range(BLOCKS):
-        targ[b] = seen[jnp.clip(table_of[3, b], 0, PATH - 1)]
+        targ[b] = seen[jnp.clip(table_of[4, b], 0, PATH - 2)]
 
     def wide(p, f):
         two = jnp.concatenate([targ[2 * p, f : f + 1, :], targ[2 * p + 1, f : f + 1, :]], axis=1)
@@ -487,26 +478,27 @@
 
     lax.fori_loop(0, WIDES, close, 0)
 
-    def expand(s, _):
-        owner = s * GAS + (lane8 >> 5)
-        begin = jnp.where(s < TILES // 2, take_lanes(begin0, owner & 127), take_lanes(begin1, owner & 127))
-        t = jnp.minimum(begin + (lane8 & (SLOTS - 1)), ACTIVE - 1)
-        block, lane = t >> 7, t & 127
-        first = jnp.clip(table_of[s >> 5, (s << 2) & 127] >> 7, 0, BLOCKS - 1)
-        second = jnp.minimum(first + 1, BLOCKS - 1)
-        ty, tz, tx = tile_at(s)
-        part[ty, tz, tx] = jnp.where(
-            block == first, take_lanes(pt[first], lane), take_lanes(pt[second], lane)
+    pt[BLOCKS] = jnp.zeros((8, 128), f32)
+    for t in range(TILES):
+        begin = take_lanes(begin0 if t < TILES // 2 else begin1, (lane8 >> 5) + ((t * GAS) & 127))
+        slot = jnp.minimum(begin + (lane8 & (SLOTS - 1)), ACTIVE - 1)
+        first = jnp.clip(table_of[t // 32, (t * GAS) & 127], 0, BLOCKS - 1)
+        lane = slot & 127
+        part[seat(t)] = jnp.where(
+            (slot >> 7) == first, take_lanes(pt[first], lane), take_lanes(pt[first + 1], lane)
         )
-        return 0
-
-    lax.fori_loop(0, TILES, expand, 0, unroll=4)
-
-    xcs = [
-        send(part.at[:, :, other], r1.at[xc], xs2.at[d], xr2.at[d], device)
-        for d, (other, device) in enumerate(xp)
+
+    away = pl.ds((1 - core) * HALF, HALF)
+    cc = send(part.at[away], r1, cs2.at[0], cr2.at[0], partner)
+
+    cc.wait()
+    q1[...] = part[pl.ds(core * HALF, HALF)] + r1[...]
+    pcs = [
+        send(q1.at[pl.ds(other * ZL, ZL)], r2.at[pi], ps2.at[d], pr2.at[d], device)
+        for d, (other, device) in enumerate(pp)
     ]
-    r1[xc] = part[:, :, xc]
+    r2[pi] = q1[pl.ds(pi * ZL, ZL)]
+    local, used = own_indices(active, star * GAS + gas, 0)
 
     for copy in hcs:
         copy.wait()
@@ -529,27 +521,15 @@
         out = 0.5 * (mag[c][4:-4] + one[c][2:-2] + field_step * second[c])
         field_out[c] = out[:, NYL : 2 * NYL, 0:NZ]
 
-    for copy in xcs:
-        copy.wait()
-    total = r1[0]
-    for n in range(1, XC):
-        total = total + r1[n]
-    q1[...] = total
-    ycs = [
-        send(q1.at[other], r2.at[y], ys2.at[d], yr2.at[d], device)
-        for d, (other, device) in enumerate(yp)
-    ]
-    r2[y] = q1[y]
-    local, used = own_indices(active, star * GAS + gas, 0)
-    for copy in ycs:
+    for copy in pcs:
         copy.wait()
     total = r2[0]
-    for n in range(1, YN):
+    for n in range(1, YN * XN):
         total = total + r2[n]
     t2[...] = total
     zcs = [
         send(t2.at[ozl], r3.at[zi], zs2.at[d], zr2.at[d], device)
-        for d, (other, ozl, device) in enumerate(zp)
+        for d, (ozl, device) in enumerate(zp)
     ]
     r3[zi] = t2[zl]
     for copy in zcs:
@@ -585,7 +565,8 @@
 def body(star_pos, star_vel, star_accel, star_mass, active, density, flow_in, field_in):
     brick = (NXL, NYL, NZ)
     zn = ZL * GAS
-    pairs = [DMA((n,)) for n in (zn - 1, zn - 1, YN - 1, YN - 1, XC - 1, XC - 1)]
+    plane = YN * XN
+    pairs = [DMA((n,)) for n in (zn - 1, zn - 1, plane - 1, plane - 1, 1, 1)]
     star_new, flow, field_out = pl.pallas_call(
         step_kernel,
         out_shape=(
@@ -606,7 +587,7 @@
             pltpu.VMEM((8, STARS), f32),
             pltpu.VMEM((8, 128), f32),
             pltpu.VMEM((zn, 8, 128), f32),
-            pltpu.VMEM((YN, ZL, XC, 8, 128), f32),
+            pltpu.VMEM((TILES, 8, 128), f32),
             pltpu.VMEM((8, 128), i32),
             pltpu.SMEM((8, 128), i32),
             pltpu.VMEM((BLOCKS, 8, 128), i32),
@@ -620,19 +601,19 @@
             pltpu.VMEM((WIDES, NZ, WIDE), f32),
             pltpu.VMEM((3, WIDES, 8, WIDE), f32),
             pltpu.VMEM((CELL_TILES, 8, WIDE), f32),
-            pltpu.VMEM((BLOCKS, 8, 128), f32),
+            pltpu.VMEM((BLOCKS + 1, 8, 128), f32),
             pltpu.VMEM((8, STARS), f32),
             pltpu.VMEM((128, 128), f32),
             pltpu.VMEM((WIDE, 2 * WIDE), bf16),
             pltpu.VMEM((WIDE, 2 * WIDE), bf16),
             pltpu.VMEM((WIDE, 2 * WIDE), bf16),
             pltpu.VMEM((WIDE, 2 * WIDE), bf16),
-            pltpu.VMEM((YN, ZL, XC, 8, 128), f32),
+            pltpu.VMEM((TILES, 8, 128), f32),
             pltpu.VMEM((3, 3, 4) + brick, f32),
             pltpu.VMEM((3, 3, 3) + brick, f32),
-            pltpu.VMEM((XC, YN, ZL, 8, 128), f32),
-            pltpu.VMEM((YN, ZL, 8, 128), f32),
-            pltpu.VMEM((YN, ZL, 8, 128), f32),
+            pltpu.VMEM((HALF, 8, 128), f32),
+            pltpu.VMEM((HALF, 8, 128), f32),
+            pltpu.VMEM((plane, ZL, 8, 128), f32),
             pltpu.VMEM((ZL, 8, 128), f32),
             pltpu.VMEM((zn, 8, 128), f32),
             pltpu.VMEM((7, 3 * NXL, 3 * NYL, 128), f32),

time: 64.8 us -> 60.3 us (0.931)
  Pallas kernels: 61.1 us -> 56.6 us
    pallas_call x1, Pallas kernels: 61.1 us -> 56.6 us  [body(): pl.pallas_call(step_kernel, out_shape=(jax.ShapeDtypeStruct((12, STARS),...]
where the time goes in v4:
time: 60.3 us; the launch traced here: 60.1 us
  Pallas kernels  56.6 us (94%)
  local copies, waits for them, and re-layouts  2.83 us (5%)
  between operations  0.65 us (1%)
    pallas_call x1, Pallas kernels, body(): pl.pallas_call(step_kernel, out_shape=(jax.ShapeDtypeStruct((12, STARS),...  56.6 us
    unnamed x7, local copies, waits for them, and re-layouts  2.83 us

profile of v4, /device:TPU:32, one launch (start us, length us, event | category | flops | bytes accessed | tf_op | source)
XLA Modules:
  0.0 60.1 jit_solution(412506342151599023)
XLA Ops:
  0.6 56.6 %block_step.1 = (f32[12,512]{1,0:T(8,128)}, f32[3,4,8,64]{3,2,1,0:T(8,128)}, f32[3,4,8,64]{3,2,1,0:T(8,128)}) custom-call(f32[3,512]{1,0:T(4,128)} %pos_in.1, f32[3,512]{1,0:T(4,128)} %vel_in.1, f32[6,512]{1,0:T(8,128)} %accel_in.1, f32[1,512]{1,0:T(1,128)} %bitcast.3, s32[16,128]{1,0:T(8,128)} %bitcast.2, f32[4,8,64]{2,1,0:T(8,128)} %density_in.1, ...), custom_call_target="tpu_custom_call" | custom-call | tf_op jit(solution)/shard_map/block_step/pallas_call | solution.py:570
  57.2 0.0 copy-start.1
  57.3 1.4 %copy.14 = f32[12,512]{1,0:T(8,128)} copy(f32[12,512]{1,0:T(8,128)} %get-tuple-element.6) | data formatting | bytes 49152
  58.6 0.0 copy-done.1
  58.6 0.0 copy-start
  58.6 0.6 %copy.15 = f32[3,4,8,64]{3,2,1,0:T(8,128)} copy(f32[3,4,8,64]{3,2,1,0:T(8,128)S(1)} %copy-done.1) | data formatting | bytes 49152
  59.3 0.2 copy-done
  59.5 0.6 %copy.16 = f32[3,4,8,64]{3,2,1,0:T(8,128)} copy(f32[3,4,8,64]{3,2,1,0:T(8,128)S(1)} %copy-done) | data formatting | bytes 49152
Async XLA Ops:
  57.2 1.4 %copy-start.1 = (f32[3,4,8,64]{3,2,1,0:T(8,128)S(1)}, f32[3,4,8,64]{3,2,1,0:T(8,128)}, u32[]{:S(2)}) copy-start(f32[3,4,8,64]{3,2,1,0:T(8,128)} %get-tuple-element.7) | copy-start | bytes 73732
  58.6 0.8 %copy-start = (f32[3,4,8,64]{3,2,1,0:T(8,128)S(1)}, f32[3,4,8,64]{3,2,1,0:T(8,128)}, u32[]{:S(2)}) copy-start(f32[3,4,8,64]{3,2,1,0:T(8,128)} %get-tuple-element.8) | copy-start | bytes 73732

commit v5 on v4

--- a/solution.py
+++ b/solution.py
@@ -27,6 +27,7 @@
 WIDES = ACTIVE // WIDE
 CELL_TILES = NXL * NYL * NZ // WIDE
 MIDDLE = 16.0
+PART = 256
 f32 = jnp.float32
 bf16 = jnp.bfloat16
 i32 = jnp.int32
@@ -121,6 +122,12 @@
     return jnp.concatenate([v, v], axis=1)
 
 
+def thirds(v):
+    high = v.astype(bf16).astype(f32)
+    mid = (v - high).astype(bf16).astype(f32)
+    return high, mid, (v - high - mid).astype(bf16).astype(f32)
+
+
 def both(v):
     hi = v.astype(bf16).astype(f32)
     return jnp.concatenate([hi, v - hi], axis=0).astype(bf16)
@@ -178,7 +185,7 @@
     pos_in, vel_in, accel_in, mass_in, active_in, density_in, flow_from, field_in,
     star_new, flow, field_out,
     pos, vel, accel, mass, active, brick, flow_in, res, own, zbuf, tiles, table, table_of,
-    spots, homes, seen, targ, rb, sm, cm, tm, dz2, mom, kacc, pt, rows8, square, wa, wb, pa, pb,
+    spots, homes, seen, targ, ls, rt, sm, cm, tm, dz2, mom, kacc, pt, rows8, square, wa, wb, pa, pb,
     part, near, wind_near, r1, q1, r2, t2, r3, big,
     ins, zs, zr, ps, pr, cs, cr, hs, hr, fs, fr, zs2, zr2, ps2, pr2, cs2, cr2
 ):
@@ -288,12 +295,21 @@
         send(tiles.at[pair], tiles.at[pair], ps.at[d], pr.at[d], device)
         for d, (other, device) in enumerate(pp)
     ]
+    away_x = res[0:3, :] - MIDDLE
+    rows8[0:3, :] = away_x
+    rows8[3:6, :] = res[3:6, :]
+    rows8[6:7, :] = jnp.sum(away_x * res[3:6, :], 0, keepdims=True)
+    rows8[7:8, :] = jnp.sum(away_x * away_x, 0, keepdims=True)
+    high, mid, low = thirds(rows8[...])
+    ones = jnp.where(lax.broadcasted_iota(i32, (8, 128), 0) < 3, 1.0, 0.0)
     square[...] = jnp.zeros((128, 128), f32)
     for q in range(STARS // 128):
-        square[0:8, :] = res[:, q * 128 : (q + 1) * 128]
-        turned = jnp.transpose(square[...])
-        for f in range(6):
-            rb[f, q * 128 : (q + 1) * 128, :] = jnp.broadcast_to(turned[:, f : f + 1], (128, 128))
+        at = slice(q * 128, (q + 1) * 128)
+        for n, part_of in enumerate((high, high, high, mid, mid, low)):
+            square[n * 8 : (n + 1) * 8, :] = part_of[:, at]
+        square[48:56, :] = ones
+        ls[at, :] = jnp.transpose(square[...]).astype(bf16)
+    square[...] = jnp.zeros((128, 128), f32)
     gm = res[6:7, :] * gravity
     rows8[0:1, :] = gm
     rows8[1:4, :] = gm * (res[0:3, :] - MIDDLE)
@@ -352,6 +368,8 @@
 
     height = lax.broadcasted_iota(i32, (NZ, WIDE), 0).astype(f32) + 0.5
 
+    row_of = lax.broadcasted_iota(i32, (8, WIDE), 0)
+
     def moments(p, _):
         gm = wide(p, 6)[0:1] * gravity
         rows8[0:1, 0:WIDE] = gm
@@ -359,6 +377,27 @@
         rows8[2:3, 0:WIDE] = gm * (wide(p, 1)[0:1] - y_mid)
         rows8[3:4, 0:WIDE] = gm * (wide(p, 2)[0:1] - z_mid)
         tm[p] = twice(both(rows8[:, 0:WIDE]))
+        block = jnp.concatenate([targ[2 * p], targ[2 * p + 1]], axis=1)
+        away = jnp.where(row_of < 3, block - MIDDLE, block)
+        swap = jnp.where(row_of < 3, pltpu.roll(away, 5, 0), pltpu.roll(away, 3, 0))
+        apart = jnp.where(row_of < 6, -swap, jnp.where(row_of == 6, 1.0, 0.0))
+        near_by = jnp.where(row_of < 3, -2.0 * away, jnp.where(row_of == 7, 1.0, 0.0))
+        factors = thirds(jnp.concatenate([apart, near_by], axis=1))
+        for n, k in enumerate((0, 1, 2, 0, 1, 0)):
+            if n % 2 == 0:
+                m = (0, 1, 2, 0, 1, 0)[n + 1]
+                rt[p, n * 8 : (n + 2) * 8, :] = jnp.concatenate(
+                    [factors[k], factors[m]], axis=0
+                ).astype(bf16)
+        first3 = row_of < 3
+        self_u = jnp.sum(jnp.where(first3, away * swap, 0.0), 0, keepdims=True)
+        self_d = jnp.sum(jnp.where(first3, away * away, 0.0), 0, keepdims=True) + soften
+        tail = thirds(jnp.broadcast_to(jnp.concatenate([self_u, self_d], axis=1), (8, 2 * WIDE)))
+        row2 = jnp.concatenate([row_of, row_of], axis=1)
+        tail = jnp.where(
+            row2 == 0, tail[0], jnp.where(row2 == 1, tail[1], jnp.where(row2 == 2, tail[2], 0.0))
+        )
+        rt[p, 48:64, :] = jnp.concatenate([tail, jnp.zeros_like(tail)], axis=0).astype(bf16)
         depth = height - jnp.broadcast_to(wide(p, 2)[0:1], (NZ, WIDE))
         dz2[p] = depth * depth
         for f in range(3):
@@ -387,7 +426,7 @@
         p, i = lax.div(step, NXL), lax.rem(step, NXL)
         q = i * 2 + half
         w = w_buf[...]
-        mom[2, p] += fold(dot_nn(cm[q], w))
+        mom[2, p] += fold(dot_nn(cm[q], w[:, 0:WIDE]))
         kacc[q] += fold(dot_nt(tm[p], w))
 
     def gas_on(step, _):
@@ -431,18 +470,18 @@
     wb[...] = jnp.zeros((WIDE, 2 * WIDE), bf16)
 
     def star_weights(p, c, w_buf, p_buf):
-        tx, ty, tz, tu, tv, tw = (jnp.concatenate([wide(p, f)] * 2, axis=0) for f in range(6))
-        for g in range(WIDE // 16):
-            at = pl.ds(c * WIDE + g * 16, 16)
-            dx, dy, dz = twice(rb[0, at, :]) - tx, twice(rb[1, at, :]) - ty, twice(rb[2, at, :]) - tz
-            ux, uy, uz = twice(rb[3, at, :]) - tu, twice(rb[4, at, :]) - tv, twice(rb[5, at, :]) - tw
-            inv = lax.rsqrt(dx * dx + dy * dy + dz * dz + soften)
-            inv2 = inv * inv
-            w = inv2 * inv
-            pull = (dx * ux + dy * uy + dz * uz) * (3.0 * inv2) * w
-            here = slice(g * 16, (g + 1) * 16)
-            w_buf[here, 0:WIDE], w_buf[here, WIDE:] = split(w)
-            p_buf[here, 0:WIDE], p_buf[here, WIDE:] = split(pull)
+        for m in range(WIDE // PART):
+            rows = slice(c * WIDE + m * PART, c * WIDE + (m + 1) * PART)
+            products = dot_nn(ls[rows, 0:64], rt[p])
+            for g in range(PART // 16):
+                at = slice(g * 16, (g + 1) * 16)
+                inv = lax.rsqrt(products[at, WIDE:])
+                inv2 = inv * inv
+                w = inv2 * inv
+                pull = products[at, 0:WIDE] * inv2 * w
+                here = slice(m * PART + g * 16, m * PART + (g + 1) * 16)
+                w_buf[here, 0:WIDE], w_buf[here, WIDE:] = split(w)
+                p_buf[here, 0:WIDE], p_buf[here, WIDE:] = split(pull)
 
     def star_sums(p, c, w_buf, p_buf):
         lhs = sm[:, c * WIDE : (c + 1) * WIDE]
@@ -459,7 +498,7 @@
     lax.fori_loop(0, WIDES, stars_on, 0)
     star_sums(WIDES - 1, 1, wb, pb)
     def close(p, _):
-        w, pull, g = mom[0, p], mom[1, p], mom[2, p]
+        w, pull, g = mom[0, p], 3.0 * mom[1, p], mom[2, p]
         mids = (x_mid, y_mid, z_mid)
         for f in range(3):
             at = wide(p, f)[0:1]
@@ -594,7 +633,8 @@
             pltpu.VMEM((BLOCKS, 8, 128), i32),
             pltpu.VMEM((PATH, 8, 128), f32),
             pltpu.VMEM((BLOCKS, 8, 128), f32),
-            pltpu.VMEM((6, STARS, 128), f32),
+            pltpu.VMEM((STARS, 128), bf16),
+            pltpu.VMEM((WIDES, 64, 2 * WIDE), bf16),
             pltpu.VMEM((16, STARS), bf16),
             pltpu.VMEM((CELL_TILES, 16, WIDE), bf16),
             pltpu.VMEM((WIDES, 16, 2 * WIDE), bf16),

time: 60.3 us -> 58.1 us (0.964)
  Pallas kernels: 56.6 us -> 54.4 us
    pallas_call x1, Pallas kernels: 56.6 us -> 54.4 us  [body(): pl.pallas_call(step_kernel, out_shape=(jax.ShapeDtypeStruct((12, STARS),...]
where the time goes in v5:
time: 58.1 us; the launch traced here: 57.9 us
  Pallas kernels  54.4 us (94%)
  local copies, waits for them, and re-layouts  2.83 us (5%)
  between operations  0.65 us (1%)
    pallas_call x1, Pallas kernels, body(): pl.pallas_call(step_kernel, out_shape=(jax.ShapeDtypeStruct((12, STARS),...  54.4 us
    unnamed x7, local copies, waits for them, and re-layouts  2.83 us

profile of v5, /device:TPU:32, one launch (start us, length us, event | category | flops | bytes accessed | tf_op | source)
XLA Modules:
  0.0 57.9 jit_solution(1730045268027145398)
XLA Ops:
  0.6 54.4 %block_step.1 = (f32[12,512]{1,0:T(8,128)}, f32[3,4,8,64]{3,2,1,0:T(8,128)}, f32[3,4,8,64]{3,2,1,0:T(8,128)}) custom-call(f32[3,512]{1,0:T(4,128)} %pos_in.1, f32[3,512]{1,0:T(4,128)} %vel_in.1, f32[6,512]{1,0:T(8,128)} %accel_in.1, f32[1,512]{1,0:T(1,128)} %bitcast.3, s32[16,128]{1,0:T(8,128)} %bitcast.2, f32[4,8,64]{2,1,0:T(8,128)} %density_in.1, ...), custom_call_target="tpu_custom_call" | custom-call | tf_op jit(solution)/shard_map/block_step/pallas_call | solution.py:609
  55.1 0.0 copy-start.1
  55.1 1.4 %copy.14 = f32[12,512]{1,0:T(8,128)} copy(f32[12,512]{1,0:T(8,128)} %get-tuple-element.6) | data formatting | bytes 49152
  56.5 0.0 copy-done.1
  56.5 0.0 copy-start
  56.5 0.6 %copy.15 = f32[3,4,8,64]{3,2,1,0:T(8,128)} copy(f32[3,4,8,64]{3,2,1,0:T(8,128)S(1)} %copy-done.1) | data formatting | bytes 49152
  57.1 0.2 copy-done
  57.3 0.6 %copy.16 = f32[3,4,8,64]{3,2,1,0:T(8,128)} copy(f32[3,4,8,64]{3,2,1,0:T(8,128)S(1)} %copy-done) | data formatting | bytes 49152
Async XLA Ops:
  55.1 1.4 %copy-start.1 = (f32[3,4,8,64]{3,2,1,0:T(8,128)S(1)}, f32[3,4,8,64]{3,2,1,0:T(8,128)}, u32[]{:S(2)}) copy-start(f32[3,4,8,64]{3,2,1,0:T(8,128)} %get-tuple-element.7) | copy-start | bytes 73732
  56.5 0.8 %copy-start = (f32[3,4,8,64]{3,2,1,0:T(8,128)S(1)}, f32[3,4,8,64]{3,2,1,0:T(8,128)}, u32[]{:S(2)}) copy-start(f32[3,4,8,64]{3,2,1,0:T(8,128)} %get-tuple-element.8) | copy-start | bytes 73732

commit v6 on v5

--- a/solution.py
+++ b/solution.py
@@ -597,8 +597,14 @@
 
 
 VM = pl.BlockSpec(memory_space=pltpu.VMEM)
-ANY = pl.BlockSpec(memory_space=pl.ANY)
+ANY = pl.BlockSpec(memory_space=pltpu.HBM)
 DMA = pltpu.SemaphoreType.DMA
+
+
+def hand_out(star_new, flow, field_out, a, b, c):
+    a[...] = star_new[...]
+    b[...] = flow[...]
+    c[...] = field_out[...]
 
 
 def body(star_pos, star_vel, star_accel, star_mass, active, density, flow_in, field_in):
@@ -606,6 +612,10 @@
     zn = ZL * GAS
     plane = YN * XN
     pairs = [DMA((n,)) for n in (zn - 1, zn - 1, plane - 1, plane - 1, 1, 1)]
+    star_pos, star_vel, star_accel, star_mass, active, density, flow_in, field_in = (
+        pltpu.with_memory_space_constraint(v, pltpu.HBM)
+        for v in (star_pos, star_vel, star_accel, star_mass.reshape(1, STARS), active.reshape(BLOCKS, 128), density, flow_in, field_in)
+    )
     star_new, flow, field_out = pl.pallas_call(
         step_kernel,
         out_shape=(
@@ -660,14 +670,21 @@
             DMA((9,)), *pairs, DMA((8,)), DMA((8,)), DMA((8,)), DMA((8,)), *pairs,
         ],
         compiler_params=pltpu.CompilerParams(
-            collective_id=0, has_side_effects=True, vmem_limit_bytes=63 << 20
+            collective_id=0, has_side_effects=True, vmem_limit_bytes=24 << 20
         ),
         name="block_step",
     )(
-        star_pos, star_vel, star_accel, star_mass.reshape(1, STARS),
-        active.reshape(BLOCKS, 128), density, flow_in, field_in,
+        star_pos, star_vel, star_accel, star_mass,
+        active, density, flow_in, field_in,
     )
-    return (star_new, flow, field_out)
+    return pl.pallas_call(
+        hand_out,
+        out_shape=tuple(jax.ShapeDtypeStruct(v.shape, f32) for v in (star_new, flow, field_out)),
+        in_specs=[VM] * 3,
+        out_specs=(VM,) * 3,
+        compiler_params=pltpu.CompilerParams(vmem_limit_bytes=24 << 20),
+        name="hand_out",
+    )(star_new, flow, field_out)
 
 
 def solution(mesh):

time: 58.1 us -> 55.2 us (0.950)
  local copies, waits for them, and re-layouts: 2.83 us -> 0 us
    unnamed x7 -> x0, local copies, waits for them, and re-layouts: 2.83 us -> none
    pallas_call x0 -> x1, Pallas kernels: none -> 0.66 us  [body(): pl.pallas_call(hand_out, out_shape=tuple((jax.ShapeDtypeStruct(v.shape, f...]
    pallas_call x1, Pallas kernels: 54.4 us -> 53.8 us  [body(): pl.pallas_call(step_kernel, out_shape=(jax.ShapeDtypeStruct((12, STARS),...]
where the time goes in v6:
time: 55.2 us; the launch traced here: 55.1 us
  Pallas kernels  54.5 us (99%)
  between operations  0.64 us (1%)
    pallas_call x1, Pallas kernels, body(): pl.pallas_call(step_kernel, out_shape=(jax.ShapeDtypeStruct((12, STARS),...  53.8 us

profile of v6, /device:TPU:32, one launch (start us, length us, event | category | flops | bytes accessed | tf_op | source)
XLA Modules:
  0.0 55.1 jit_solution(13026513770051892232)
XLA Ops:
  0.6 53.8 %block_step.1 = (f32[12,512]{1,0:T(8,128)S(1)}, f32[3,4,8,64]{3,2,1,0:T(8,128)S(1)}, f32[3,4,8,64]{3,2,1,0:T(8,128)S(1)}) custom-call(f32[3,512]{1,0:T(4,128)} %pos_in.1, f32[3,512]{1,0:T(4,128)} %vel_in.1, f32[6,512]{1,0:T(8,128)} %accel_in.1, f32[1,512]{1,0:T(1,128)} %bitcast.3, s32[16,128]{1,0:T(8,128)} %bitcast.2, f32[4,8,64]{2,1,0:T(8,128)} %density_in.1, ...), custom_call_target="tpu_custom_call" | custom-call | tf_op jit(solution)/shard_map/block_step/pallas_call | solution.py:619
  54.4 0.7 %hand_out.1 = (f32[12,512]{1,0:T(8,128)}, f32[3,4,8,64]{3,2,1,0:T(8,128)}, f32[3,4,8,64]{3,2,1,0:T(8,128)}) custom-call(f32[12,512]{1,0:T(8,128)S(1)} %get-tuple-element.6.star_new, f32[3,4,8,64]{3,2,1,0:T(8,128)S(1)} %get-tuple-element.7.flow, f32[3,4,8,64]{3,2,1,0:T(8,128)S(1)} %get-tuple-element.8.field_out), custom_call_target="tpu_custom_call" | custom-call | tf_op jit(solution)/shard_map/hand_out/pallas_call | solution.py:680

commit v7 on v6

--- a/solution.py
+++ b/solution.py
@@ -518,17 +518,24 @@
     lax.fori_loop(0, WIDES, close, 0)
 
     pt[BLOCKS] = jnp.zeros((8, 128), f32)
-    for t in range(TILES):
-        begin = take_lanes(begin0 if t < TILES // 2 else begin1, (lane8 >> 5) + ((t * GAS) & 127))
-        slot = jnp.minimum(begin + (lane8 & (SLOTS - 1)), ACTIVE - 1)
-        first = jnp.clip(table_of[t // 32, (t * GAS) & 127], 0, BLOCKS - 1)
-        lane = slot & 127
-        part[seat(t)] = jnp.where(
-            (slot >> 7) == first, take_lanes(pt[first], lane), take_lanes(pt[first + 1], lane)
-        )
+
+    def expand(bit):
+        for k in range(HALF):
+            owner = (k * CORES * GAS) % 128 + bit * GAS
+            half = k * CORES * GAS // 128
+            begin = take_lanes(begin1 if half else begin0, (lane8 >> 5) + owner)
+            slot = jnp.minimum(begin + (lane8 & (SLOTS - 1)), ACTIVE - 1)
+            first = jnp.clip(table_of[half, owner], 0, BLOCKS - 1)
+            lane = slot & 127
+            part[bit * HALF + seat(k * CORES)] = jnp.where(
+                (slot >> 7) == first, take_lanes(pt[first], lane), take_lanes(pt[first + 1], lane)
+            )
+
+    expand(1 - core)
 
     away = pl.ds((1 - core) * HALF, HALF)
     cc = send(part.at[away], r1, cs2.at[0], cr2.at[0], partner)
+    expand(core)
 
     cc.wait()
     q1[...] = part[pl.ds(core * HALF, HALF)] + r1[...]
@@ -560,6 +567,12 @@
         out = 0.5 * (mag[c][4:-4] + one[c][2:-2] + field_step * second[c])
         field_out[c] = out[:, NYL : 2 * NYL, 0:NZ]
 
+    index = lanes((8, STARS))
+    source = jnp.full((8, STARS), -1, i32)
+    for n in range(MOST):
+        source = jnp.where(index == local[:, n : n + 1], n, source)
+    is_active = source[0:3] >= 0
+    source = jnp.where(source >= 0, source + gas * SLOTS, 0)
     for copy in pcs:
         copy.wait()
     total = r2[0]
@@ -576,15 +589,9 @@
     total = r3[0]
     for n in range(1, ZL * GAS):
         total = total + r3[n]
-    mine = pltpu.roll(total, lax.rem(128 - gas * SLOTS, 128), 1)
-    index = lanes((8, STARS))
-    sums = jnp.zeros((8, STARS), f32)
-    hit = jnp.zeros((8, STARS), f32)
-    for s in range(MOST):
-        here = index == local[:, s : s + 1]
-        sums = jnp.where(here, mine[:, s : s + 1], sums)
-        hit = jnp.where(here, 1.0, hit)
-    is_active = hit[0:3] > 0.5
+    sums = jnp.concatenate(
+        [take_lanes(total, source[:, b * 128 : (b + 1) * 128]) for b in range(STARS // 128)], axis=1
+    )
     new_acc, new_jerk = sums[0:3], sums[3:6]
     p, v = pos[...], vel[...]
     old_acc, old_jerk = accel[0:3, :], accel[3:6, :]

time: 55.2 us -> 54 us (0.978)
  Pallas kernels: 54.5 us -> 53 us
    pallas_call x1, Pallas kernels: 53.8 us -> 52.4 us  [body(): pl.pallas_call(step_kernel, out_shape=(jax.ShapeDtypeStruct((12, STARS),...]
where the time goes in v7:
time: 54 us; the launch traced here: 53.7 us
  Pallas kernels  53 us (98%)
  between operations  0.64 us (1%)
    pallas_call x1, Pallas kernels, body(): pl.pallas_call(step_kernel, out_shape=(jax.ShapeDtypeStruct((12, STARS),...  52.4 us

profile of v7, /device:TPU:32, one launch (start us, length us, event | category | flops | bytes accessed | tf_op | source)
XLA Modules:
  0.0 53.7 jit_solution(16143279345706569431)
XLA Ops:
  0.6 52.4 %block_step.1 = (f32[12,512]{1,0:T(8,128)S(1)}, f32[3,4,8,64]{3,2,1,0:T(8,128)S(1)}, f32[3,4,8,64]{3,2,1,0:T(8,128)S(1)}) custom-call(f32[3,512]{1,0:T(4,128)} %pos_in.1, f32[3,512]{1,0:T(4,128)} %vel_in.1, f32[6,512]{1,0:T(8,128)} %accel_in.1, f32[1,512]{1,0:T(1,128)} %bitcast.3, s32[16,128]{1,0:T(8,128)} %bitcast.2, f32[4,8,64]{2,1,0:T(8,128)} %density_in.1, ...), custom_call_target="tpu_custom_call" | custom-call | tf_op jit(solution)/shard_map/block_step/pallas_call | solution.py:626
  53.0 0.7 %hand_out.1 = (f32[12,512]{1,0:T(8,128)}, f32[3,4,8,64]{3,2,1,0:T(8,128)}, f32[3,4,8,64]{3,2,1,0:T(8,128)}) custom-call(f32[12,512]{1,0:T(8,128)S(1)} %get-tuple-element.6.star_new, f32[3,4,8,64]{3,2,1,0:T(8,128)S(1)} %get-tuple-element.7.flow, f32[3,4,8,64]{3,2,1,0:T(8,128)S(1)} %get-tuple-element.8.field_out), custom_call_target="tpu_custom_call" | custom-call | tf_op jit(solution)/shard_map/hand_out/pallas_call | solution.py:687

commit v8 on v7

--- a/solution.py
+++ b/solution.py
@@ -62,20 +62,21 @@
 def z_peers(y, zl, x, core, gas):
     zi = zl * GAS + gas
     peers = []
-    for d in range(1, ZL * GAS):
-        other = lax.rem(zi + d, ZL * GAS)
-        ozl, ogas = lax.div(other, GAS), lax.rem(other, GAS)
+    z, n = gas * ZL + zl, ZL * GAS
+    for d in sorted(range(1, n), key=lambda d: -min(d, n - d)):
+        other = lax.rem(z + d, n)
+        ozl, ogas = lax.rem(other, ZL), lax.div(other, ZL)
         peers.append((ozl, (star_of(y, ozl, x, core), ogas)))
     return zi, peers
 
 
 def plane_peers(y, zl, x, core, gas):
     peers = []
-    for dy in range(YN):
-        for dx in range(XN):
-            if dy or dx:
-                oy, ox = lax.rem(y + dy, YN), lax.rem(x + dx, XN)
-                peers.append((oy * XN + ox, (star_of(oy, zl, ox, core), gas)))
+    steps = [(dy, dx) for dy in range(YN) for dx in range(XN) if dy or dx]
+    steps.sort(key=lambda s: -min(s[0], YN - s[0]) - min(s[1], XN - s[1]))
+    for dy, dx in steps:
+        oy, ox = lax.rem(y + dy, YN), lax.rem(x + dx, XN)
+        peers.append((oy * XN + ox, (star_of(oy, zl, ox, core), gas)))
     return y * XN + x, peers
 
 

time: 54 us -> 53.1 us (0.983)
  Pallas kernels: 53 us -> 52.1 us
    pallas_call x1, Pallas kernels: 52.4 us -> 51.5 us  [body(): pl.pallas_call(step_kernel, out_shape=(jax.ShapeDtypeStruct((12, STARS),...]
where the time goes in v8:
time: 53.1 us; the launch traced here: 52.8 us
  Pallas kernels  52.1 us (98%)
  between operations  0.64 us (1%)
    pallas_call x1, Pallas kernels, body(): pl.pallas_call(step_kernel, out_shape=(jax.ShapeDtypeStruct((12, STARS),...  51.5 us

profile of v8, /device:TPU:32, one launch (start us, length us, event | category | flops | bytes accessed | tf_op | source)
XLA Modules:
  0.0 52.8 jit_solution(5106061124842811857)
XLA Ops:
  0.6 51.5 %block_step.1 = (f32[12,512]{1,0:T(8,128)S(1)}, f32[3,4,8,64]{3,2,1,0:T(8,128)S(1)}, f32[3,4,8,64]{3,2,1,0:T(8,128)S(1)}) custom-call(f32[3,512]{1,0:T(4,128)} %pos_in.1, f32[3,512]{1,0:T(4,128)} %vel_in.1, f32[6,512]{1,0:T(8,128)} %accel_in.1, f32[1,512]{1,0:T(1,128)} %bitcast.3, s32[16,128]{1,0:T(8,128)} %bitcast.2, f32[4,8,64]{2,1,0:T(8,128)} %density_in.1, ...), custom_call_target="tpu_custom_call" | custom-call | tf_op jit(solution)/shard_map/block_step/pallas_call | solution.py:627
  52.1 0.7 %hand_out.1 = (f32[12,512]{1,0:T(8,128)}, f32[3,4,8,64]{3,2,1,0:T(8,128)}, f32[3,4,8,64]{3,2,1,0:T(8,128)}) custom-call(f32[12,512]{1,0:T(8,128)S(1)} %get-tuple-element.6.star_new, f32[3,4,8,64]{3,2,1,0:T(8,128)S(1)} %get-tuple-element.7.flow, f32[3,4,8,64]{3,2,1,0:T(8,128)S(1)} %get-tuple-element.8.field_out), custom_call_target="tpu_custom_call" | custom-call | tf_op jit(solution)/shard_map/hand_out/pallas_call | solution.py:688
